TPU v7x, 32 devices: a whole 2x2x4 slice. The times are simulated.
32 devices in a mesh: gy: 8 (over y, x, core), gz: 4 (over z).
Axes of the slice: x: 2, y: 2, z: 4, core: 2. Of those that a mesh axis runs over, the one named last changes fastest.
Arguments:
- volume: float32 [64, 128, 1024], P('gz', None, 'gy'), may hold values from -6 to 6
- contrast: float32 [128], replicated, may hold values from 0.1 to 1
Outputs:
- filtered: float32 [64, 128, 1024], P('gz', None, 'gy')
All inputs are finite; a program needn't handle non-finite values.
Results may differ from a plain program's by a relative error of at most 0.0003.
Values sent between devices are 32-bit elements; how exact they have to be, the bound alone decides.
A program may use at most 192 MiB of HBM per device.

v0:
```python
import jax
import jax.numpy as jnp
from jax import lax
from jax.sharding import PartitionSpec as P

STEPS = 2


kernel_taps = (0.05448868, 0.24420134, 0.40261995, 0.24420134, 0.05448868)
half_scale = 600.0


def extended(block, sides, width):
    for axis, dim in sides:
        count = lax.axis_size(axis)
        forward = [(i, i + 1) for i in range(count - 1)]
        backward = [(target, source) for source, target in forward]
        low = lax.ppermute(
            lax.slice_in_dim(block, block.shape[dim] - width, None, axis=dim), axis, forward
        )
        high = lax.ppermute(lax.slice_in_dim(block, 0, width, axis=dim), axis, backward)
        block = jnp.concatenate([low, block, high], axis=dim)
    return block


def slice_axis(array, start, count, axis, stride=1):
    return lax.slice_in_dim(array, start, start + stride * (count - 1) + 1, stride, axis)


def reduce_solve(lower, diagonal, upper, right, axis):
    length = right.shape[axis]
    if length == 1:
        return right / diagonal
    count_even = (length + 1) // 2
    count_odd = length // 2
    evens = [slice_axis(array, 0, count_even, axis, 2) for array in (lower, diagonal, upper, right)]
    odds = [slice_axis(array, 1, count_odd, axis, 2) for array in (lower, diagonal, upper, right)]
    before = [slice_axis(array, 0, count_odd, axis) for array in evens]
    fills = [0.0, 1.0, 0.0, 0.0]
    after = [
        slice_axis(
            jnp.concatenate([array, jnp.zeros_like(slice_axis(array, 0, 1, axis)) + extra], axis),
            1,
            count_odd,
            axis,
        )
        for array, extra in zip(evens, fills)
    ]
    factor_before = -odds[0] / before[1]
    factor_after = -odds[2] / after[1]
    new_lower = factor_before * before[0]
    new_diag = odds[1] + factor_before * before[2] + factor_after * after[0]
    new_upper = factor_after * after[2]
    new_right = odds[3] + factor_before * before[3] + factor_after * after[3]
    solved_odd = reduce_solve(new_lower, new_diag, new_upper, new_right, axis)
    zero_row = jnp.zeros_like(slice_axis(solved_odd, 0, 1, axis))
    extra_rows = [zero_row] * (count_even - count_odd)
    padded_odd = jnp.concatenate([zero_row, solved_odd] + extra_rows, axis)
    left_value = slice_axis(padded_odd, 0, count_even, axis)
    right_value = slice_axis(padded_odd, 1, count_even, axis)
    solved_even = (evens[3] - evens[0] * left_value - evens[2] * right_value) / evens[1]
    odd_full = jnp.concatenate([solved_odd] + extra_rows, axis)
    paired = jnp.stack([solved_even, odd_full], axis=axis + 1)
    shape = right.shape[:axis] + (2 * count_even,) + right.shape[axis + 1 :]
    return slice_axis(paired.reshape(shape), 0, length, axis)


def line_solve(upper, right, axis):
    length = upper.shape[axis]
    lower = jnp.concatenate(
        [jnp.zeros_like(slice_axis(upper, 0, 1, axis)), slice_axis(upper, 0, length - 1, axis)],
        axis,
    )
    diagonal = 1.0 + lower + upper
    return reduce_solve(-lower, diagonal, -upper, right, axis)


def smooth_axis(padded, axis):
    count = padded.shape[axis] - 4
    total = kernel_taps[0] * slice_axis(padded, 0, count, axis)
    for offset in range(1, 5):
        total = total + kernel_taps[offset] * slice_axis(padded, offset, count, axis)
    return total


def on_device(volume, contrast):
    depth, rows, cols = volume.shape
    count_z = lax.axis_size("gz")
    count_y = lax.axis_size("gy")
    total_z = depth * count_z
    total_y = cols * count_y
    start_z = lax.axis_index("gz") * depth
    start_y = lax.axis_index("gy") * cols
    pos_z = start_z - 2 + jnp.arange(depth + 4)
    pos_y = start_y - 2 + jnp.arange(cols + 4)
    inside = ((pos_z >= 0) & (pos_z < total_z))[:, None, None] & ((pos_y >= 0) & (pos_y < total_y))[
        None, None, :
    ]
    own_z = start_z + jnp.arange(depth) < total_z - 1
    own_y = start_y + jnp.arange(cols) < total_y - 1
    contrast_squared = (contrast * contrast)[None, :, None]
    current = volume
    for repeat in range(STEPS):
        padded = extended(current, (("gy", 2), ("gz", 0)), 4)
        blurred = smooth_axis(padded, 0)
        blurred = smooth_axis(blurred, 2)
        blurred = smooth_axis(jnp.pad(blurred, ((0, 0), (2, 2), (0, 0))), 1)
        blurred = jnp.where(inside, blurred, 0.0)
        grad_z = (blurred[2:, :, 1:-1] - blurred[:-2, :, 1:-1]) * 0.5
        grad_y = (blurred[1:-1, :, 2:] - blurred[1:-1, :, :-2]) * 0.5
        widened = jnp.pad(blurred[1:-1, :, 1:-1], ((0, 0), (1, 1), (0, 0)))
        grad_x = (widened[:, 2:] - widened[:, :-2]) * 0.5
        square = grad_x * grad_x + grad_y * grad_y + grad_z * grad_z
        diffusivity = 1.0 / (1.0 + square / contrast_squared)
        center = diffusivity[1:-1, :, 1:-1]
        face_x = jnp.concatenate(
            [(center[:, :-1] + center[:, 1:]) * half_scale, jnp.zeros_like(center[:, :1])], 1
        )
        face_y = jnp.where(
            own_y[None, None, :], (center + diffusivity[1:-1, :, 2:]) * half_scale, 0.0
        )
        face_z = jnp.where(
            own_z[:, None, None], (center + diffusivity[2:, :, 1:-1]) * half_scale, 0.0
        )
        solved_x = line_solve(face_x, current, 1)
        lined_y = line_solve(
            lax.all_to_all(face_y, "gy", split_axis=1, concat_axis=2, tiled=True),
            lax.all_to_all(current, "gy", split_axis=1, concat_axis=2, tiled=True),
            2,
        )
        solved_y = lax.all_to_all(lined_y, "gy", split_axis=2, concat_axis=1, tiled=True)
        lined_z = line_solve(
            lax.all_to_all(face_z, "gz", split_axis=1, concat_axis=0, tiled=True),
            lax.all_to_all(current, "gz", split_axis=1, concat_axis=0, tiled=True),
            0,
        )
        solved_z = lax.all_to_all(lined_z, "gz", split_axis=0, concat_axis=1, tiled=True)
        current = (solved_x + solved_y + solved_z) / 3.0
    return current


def solution(mesh):
    in_specs = (P("gz", None, "gy"), P())
    out_specs = P("gz", None, "gy")
    return jax.shard_map(
        on_device, mesh=mesh, in_specs=in_specs, out_specs=out_specs, check_vma=False
    )
```

profile of v0, /device:TPU:0, one launch (start us, length us, event | category | flops | bytes accessed | tf_op | source)
XLA Modules:
  0.0 528.2 jit_solution(7200915971150292406)
XLA Ops:
  2.9 5.2 all-to-all-start
  57.0 15.8 %all-to-all-start.1 = ((f32[16,128,128]{2,0,1:T(8,128)}), f32[16,128,128]{2,0,1:T(8,128)S(1)}, u32[]{:S(2)}, u32[]{:S(2)}) async-start(f32[16,128,128]{2,0,1:T(8,128)} %get-tuple-element.61), calls=%async_computation.1 | async-start | bytes 2097152 | tf_op jit(solution)/shard_map/all_to_all | solution.py:127
  73.6 6.2 %copy.1330 = f32[16,16,8,128]{1,0,3,2:T(8,128)} copy(f32[16,16,8,128]{3,0,1,2:T(8,128)} %bitcast.28) | data formatting | bytes 2097152 | tf_op jit(solution)/shard_map/all_to_all | solution.py:128
  97.6 7.2 %slice.2599 = f32[16,16,1023]{1,0,2:T(8,128)} slice(f32[16,16,1024]{1,0,2:T(8,128)} %bitcast.296), slice={[0:16], [0:16], [0:1023]} | slice | bytes 2095104 | tf_op jit(solution)/shard_map/slice | solution.py:27
  104.8 11.4 %bitcast_negate_fusion.3 = (f32[16,16,1024]{1,0,2:T(8,128)}, f32[16,16,1024]{1,0,2:T(8,128)S(1)}, f32[16,16,1024]{1,0,2:T(8,128)}) fusion(f32[16,16,8,128]{1,0,3,2:T(8,128)} %copy.1331, f32[16,16,1023]{1,0,2:T(8,128)} %slice.2599), kind=kLoop, calls=%fused_computation.938 | loop fusion | flops 1048576 | bytes 5241856 | tf_op jit(solution)/shard_map/neg | solution.py:75
  118.7 5.3 copy-done.1
  126.6 20.4 %fusion.2 = (f32[16,16,512]{1,0,2:T(8,128)}, f32[16,16,512]{1,0,2:T(8,128)}, f32[16,16,512]{1,0,2:T(8,128)}, f32[16,16,512]{1,0,2:T(8,128)}) fusion(f32[16,16,512]{1,0,2:T(8,128)} %slice.2057, f32[16,16,1024]{1,0,2:T(8,128)} %bitcast.299, f32[16,16,1024]{1,0,2:T(8,128)S(1)} %get-tuple-element.34, f32[16,16,1024]{1,0,2:T(8,128)} %get-tuple-element.35, ...), kind=kLoop, calls=%fused_computation.18 | loop fusion | flops 1835008 | bytes 7340032 | tf_op jit(solution)/shard_map/add | solution.py:54
  147.0 5.3 fusion.5
  158.6 6.8 %fusion.60 = (f32[16,16,256]{1,0,2:T(8,128)}, f32[16,16,256]{1,0,2:T(8,128)S(1)}, f32[16,16,256]{1,0,2:T(8,128)S(1)}, f32[16,16,256]{1,0,2:T(8,128)}) fusion(f32[16,16,256]{1,0,2:T(8,128)} %slice.2068, f32[16,16,512]{1,0,2:T(8,128)S(1)} %copy-done.8, f32[16,16,512]{1,0,2:T(8,128)S(1)} %copy-done.4, f32[16,16,512]{1,0,2:T(8,128)S(1)} %copy-done.5, ...), kind=kLoop, calls=%fused_computation.120 | loop fusion | flops 917504 | bytes 3670016 | tf_op jit(solution)/shard_map/add | solution.py:54
  172.9 5.7 %fusion.82 = (f32[16,16,128]{1,0,2:T(8,128)}, f32[16,16,128]{1,0,2:T(8,128)S(1)}, f32[16,16,128]{1,0,2:T(8,128)}, f32[16,16,128]{1,0,2:T(8,128)}) fusion(f32[16,16,128]{1,0,2:T(8,128)} %slice.2080, f32[16,16,256]{1,0,2:T(8,128)} %get-tuple-element.25, f32[16,16,256]{1,0,2:T(8,128)S(1)} %get-tuple-element.26, f32[16,16,256]{1,0,2:T(8,128)S(1)} %get-tuple-element.31, ...), kind=kLoop, calls=%fused_computation.156 | loop fusion | flops 458752 | bytes 1835008 | tf_op jit(solution)/shard_map/add | solution.py:54
  198.5 5.9 %fusion.10 = f32[16,16,512,1]{1,0,2,3:T(8,128)S(1)} fusion(f32[16,16,512]{1,0,2:T(8,128)S(1)} %bitcast.304, f32[16,16,1024]{1,0,2:T(8,128)} %bitcast.300, f32[16,16,1024]{1,0,2:T(8,128)} %get-tuple-element.33, f32[16,16,1024]{1,0,2:T(8,128)S(1)} %bitcast.293, f32[16,16,1024]{1,0,2:T(8,128)} %get-tuple-element.35), kind=kLoop, calls=%fused_computation.26 | loop fusion | flops 655360 | bytes 3145728 | tf_op jit(solution)/shard_map/stack | solution.py:63
  209.7 8.1 %reshape.239 = f32[8,1,32768]{2,1,0:T(1,128)} reshape(f32[1024,16,16]{2,1,0:T(8,128)} %bitcast.310) | data formatting | bytes 2097152
  230.8 9.0 %all-to-all-done.2 = f32[8,1,32768]{2,1,0:T(1,128)} async-done(((f32[8,1,32768]{2,1,0:T(1,128)}), f32[8,1,32768]{2,1,0:T(1,128)}, u32[]{:S(2)}, u32[]{:S(2)}) %all-to-all-start.2) | async-done | bytes 1048608 | tf_op jit(solution)/shard_map/all_to_all | solution.py:131
  239.9 5.5 %all-to-all-start.5 = ((f32[64,32,128]{2,1,0:T(8,128)}), f32[64,32,128]{2,1,0:T(8,128)S(1)}, u32[]{:S(2)}, u32[]{:S(2)}) async-start(f32[64,32,128]{2,1,0:T(8,128)} %bitcast.92), calls=%async_computation.5 | async-start | bytes 2097152 | tf_op jit(solution)/shard_map/all_to_all | solution.py:137
  254.4 6.2 %reshape.240 = f32[1024,16,16]{2,1,0:T(8,128)} reshape(f32[8,32768]{1,0:T(8,128)S(1)} %reduce) | data formatting | bytes 2097152
  260.5 5.7 %copy.1261 = f32[16,8,16,128]{3,0,2,1:T(8,128)S(1)} copy(f32[16,8,16,128]{2,0,3,1:T(8,128)} %bitcast.308) | data formatting | bytes 2097152 | tf_op jit(solution)/shard_map/all_to_all | solution.py:131
  275.8 5.2 collective-permute-done.5
  331.4 6.2 %copy.1337 = f32[16,16,8,128]{1,0,3,2:T(8,128)} copy(f32[16,16,8,128]{3,0,1,2:T(8,128)} %bitcast.124) | data formatting | bytes 2097152 | tf_op jit(solution)/shard_map/all_to_all | solution.py:128
  350.3 5.1 copy.1338
  355.3 7.2 %slice.2645 = f32[16,16,1023]{1,0,2:T(8,128)} slice(f32[16,16,1024]{1,0,2:T(8,128)} %bitcast.297), slice={[0:16], [0:16], [0:1023]} | slice | bytes 2095104 | tf_op jit(solution)/shard_map/slice | solution.py:27
  362.6 11.4 %bitcast_negate_fusion.1 = (f32[16,16,1024]{1,0,2:T(8,128)}, f32[16,16,1024]{1,0,2:T(8,128)S(1)}, f32[16,16,1024]{1,0,2:T(8,128)}) fusion(f32[16,16,8,128]{1,0,3,2:T(8,128)} %copy.1338, f32[16,16,1023]{1,0,2:T(8,128)} %slice.2645), kind=kLoop, calls=%fused_computation.936 | loop fusion | flops 1048576 | bytes 5241856 | tf_op jit(solution)/shard_map/neg | solution.py:75
  376.5 5.3 copy-done.3
  384.3 20.4 %fusion.13 = (f32[16,16,512]{1,0,2:T(8,128)}, f32[16,16,512]{1,0,2:T(8,128)}, f32[16,16,512]{1,0,2:T(8,128)}, f32[16,16,512]{1,0,2:T(8,128)}) fusion(f32[16,16,512]{1,0,2:T(8,128)} %slice.2371, f32[16,16,1024]{1,0,2:T(8,128)} %bitcast.302, f32[16,16,1024]{1,0,2:T(8,128)S(1)} %get-tuple-element.30, f32[16,16,1024]{1,0,2:T(8,128)} %get-tuple-element.36, ...), kind=kLoop, calls=%fused_computation.29 | loop fusion | flops 1835008 | bytes 7340032 | tf_op jit(solution)/shard_map/add | solution.py:54
  404.8 5.3 fusion.16
  416.3 7.0 %fusion.71 = (f32[16,16,256]{1,0,2:T(8,128)}, f32[16,16,256]{1,0,2:T(8,128)S(1)}, f32[16,16,256]{1,0,2:T(8,128)S(1)}, f32[16,16,256]{1,0,2:T(8,128)}) fusion(f32[16,16,256]{1,0,2:T(8,128)} %slice.2382, f32[16,16,512]{1,0,2:T(8,128)S(1)} %copy-done.9, f32[16,16,512]{1,0,2:T(8,128)S(1)} %copy-done.6, f32[16,16,512]{1,0,2:T(8,128)S(1)} %copy-done.7, ...), kind=kLoop, calls=%fused_computation.131 | loop fusion | flops 917504 | bytes 3670016 | tf_op jit(solution)/shard_map/add | solution.py:54
  430.9 5.7 %fusion.93 = (f32[16,16,128]{1,0,2:T(8,128)}, f32[16,16,128]{1,0,2:T(8,128)S(1)}, f32[16,16,128]{1,0,2:T(8,128)}, f32[16,16,128]{1,0,2:T(8,128)}) fusion(f32[16,16,128]{1,0,2:T(8,128)} %slice.2394, f32[16,16,256]{1,0,2:T(8,128)} %get-tuple-element.23, f32[16,16,256]{1,0,2:T(8,128)S(1)} %get-tuple-element.24, f32[16,16,256]{1,0,2:T(8,128)S(1)} %get-tuple-element.27, ...), kind=kLoop, calls=%fused_computation.167 | loop fusion | flops 458752 | bytes 1835008 | tf_op jit(solution)/shard_map/add | solution.py:54
  456.5 5.9 %fusion.21 = f32[16,16,512,1]{1,0,2,3:T(8,128)S(1)} fusion(f32[16,16,512]{1,0,2:T(8,128)S(1)} %bitcast.306, f32[16,16,1024]{1,0,2:T(8,128)} %bitcast.303, f32[16,16,1024]{1,0,2:T(8,128)} %get-tuple-element.29, f32[16,16,1024]{1,0,2:T(8,128)S(1)} %bitcast.295, f32[16,16,1024]{1,0,2:T(8,128)} %get-tuple-element.36), kind=kLoop, calls=%fused_computation.37 | loop fusion | flops 655360 | bytes 3145728 | tf_op jit(solution)/shard_map/stack | solution.py:63
  467.7 8.1 %reshape.241 = f32[8,1,32768]{2,1,0:T(1,128)} reshape(f32[1024,16,16]{2,1,0:T(8,128)} %bitcast.311) | data formatting | bytes 2097152
  489.0 9.0 %all-to-all-done.8 = f32[8,1,32768]{2,1,0:T(1,128)} async-done(((f32[8,1,32768]{2,1,0:T(1,128)}), f32[8,1,32768]{2,1,0:T(1,128)}, u32[]{:S(2)}, u32[]{:S(2)}) %all-to-all-start.8) | async-done | bytes 1048608 | tf_op jit(solution)/shard_map/all_to_all | solution.py:131
  498.0 5.1 all-to-all-start.11
  511.6 6.2 %reshape.242 = f32[1024,16,16]{2,1,0:T(8,128)} reshape(f32[8,32768]{1,0:T(8,128)S(1)} %reduce.1) | data formatting | bytes 2097152
  517.8 5.7 %copy.1316 = f32[16,8,16,128]{3,0,2,1:T(8,128)S(1)} copy(f32[16,8,16,128]{2,0,3,1:T(8,128)} %bitcast.309) | data formatting | bytes 2097152 | tf_op jit(solution)/shard_map/all_to_all | solution.py:131
  (565 shorter events, 276.4 us)
Async XLA Ops:
  2.9 54.1 %all-to-all-start = ((f32[16,128,128]{2,0,1:T(8,128)}), f32[16,128,128]{2,0,1:T(8,128)}, u32[]{:S(2)}, u32[]{:S(2)}) async-start(f32[16,128,128]{2,0,1:T(8,128)} %copy.1217), calls=%async_computation | async-start | bytes 2097152 | tf_op jit(solution)/shard_map/all_to_all | solution.py:128
  8.8 6.1 %collective-permute-start.1 = (f32[16,128,4]{1,0,2:T(8,128)S(1)}, f32[16,128,4]{1,0,2:T(8,128)S(1)}, u32[]{:S(2)}, u32[]{:S(2)}) collective-permute-start(f32[16,128,4]{1,0,2:T(8,128)S(1)} %copy.1344), channel_id=1, source_target_pairs={{4,0},{8,4},{12,8},{16,12},{20,16},{24,20},{28,24},{5,1},{9,5},{13... | collective-permute-start | bytes 98312 | tf_op jit(solution)/shard_map/ppermute | solution.py:21
  10.4 3.9 collective-permute-start
  13.5 41.3 %copy-start.69 = (pred[16]{0:T(512)(128)(4,1)}, pred[16]{0:T(512)(128)(4,1)S(1)}, u32[]{:S(2)}) copy-start(pred[16]{0:T(512)(128)(4,1)S(1)} %add_compare_fusion) | copy-start | bytes 52
  13.5 41.3 %copy-start.71 = (pred[128]{0:T(512)(128)(4,1)}, pred[128]{0:T(512)(128)(4,1)S(1)}, u32[]{:S(2)}) copy-start(pred[128]{0:T(512)(128)(4,1)S(1)} %add_compare_fusion.1) | copy-start | bytes 388
  17.5 10.7 %collective-permute-start.2 = (f32[4,128,136]{2,0,1:T(4,128)S(1)}, f32[4,128,136]{2,0,1:T(4,128)S(1)}, u32[]{:S(2)}, u32[]{:S(2)}) collective-permute-start(f32[4,128,136]{2,0,1:T(4,128)S(1)} %get-tuple-element.63), channel_id=1, source_target_pairs={{0,1},{1,2},{2,3},{4,5},{5,6},{6,7},{8,9},{9,10},{10,11},{12,13},{... | collective-permute-start | bytes 835592 | tf_op jit(solution)/shard_map/ppermute | solution.py:18
  21.5 11.1 %collective-permute-start.3 = (f32[4,128,136]{2,0,1:T(4,128)S(1)}, f32[4,128,136]{2,0,1:T(4,128)S(1)}, u32[]{:S(2)}, u32[]{:S(2)}) collective-permute-start(f32[4,128,136]{2,0,1:T(4,128)S(1)} %get-tuple-element.64), channel_id=1, source_target_pairs={{1,0},{2,1},{3,2},{5,4},{6,5},{7,6},{9,8},{10,9},{11,10},{13,12},{... | collective-permute-start | bytes 835592 | tf_op jit(solution)/shard_map/ppermute | solution.py:21
  24.2 22.2 %copy-start.73 = (f32[128]{0:T(128)}, f32[128]{0:T(128)S(1)}, u32[]{:S(2)}) copy-start(f32[128]{0:T(128)S(1)} %mul.1232) | copy-start | bytes 1540
  24.3 19.1 %copy-start.67 = (pred[20,132]{1,0:T(8,128)(4,1)}, pred[20,132]{1,0:T(8,128)(4,1)S(1)}, u32[]{:S(2)}) copy-start(pred[20,132]{1,0:T(8,128)(4,1)S(1)} %broadcast_and_fusion) | copy-start | bytes 7924
  57.0 31.2 %all-to-all-start.1 = ((f32[16,128,128]{2,0,1:T(8,128)}), f32[16,128,128]{2,0,1:T(8,128)S(1)}, u32[]{:S(2)}, u32[]{:S(2)}) async-start(f32[16,128,128]{2,0,1:T(8,128)} %get-tuple-element.61), calls=%async_computation.1 | async-start | bytes 2097152 | tf_op jit(solution)/shard_map/all_to_all | solution.py:127
  88.3 100.8 %all-to-all-start.3 = ((f32[16,128,128]{2,0,1:T(8,128)}), f32[16,128,128]{2,0,1:T(8,128)}, u32[]{:S(2)}, u32[]{:S(2)}) async-start(f32[16,128,128]{2,0,1:T(8,128)} %copy.1217), calls=%async_computation.3 | async-start | bytes 2097152 | tf_op jit(solution)/shard_map/all_to_all | solution.py:134
  189.0 31.2 %all-to-all-start.4 = ((f32[16,128,128]{2,0,1:T(8,128)}), f32[16,128,128]{2,0,1:T(8,128)}, u32[]{:S(2)}, u32[]{:S(2)}) async-start(f32[16,128,128]{2,0,1:T(8,128)} %get-tuple-element.62), calls=%async_computation.4 | async-start | bytes 2097152 | tf_op jit(solution)/shard_map/all_to_all | solution.py:133
  220.2 19.7 %all-to-all-start.2 = ((f32[8,1,32768]{2,1,0:T(1,128)}), f32[8,1,32768]{2,1,0:T(1,128)}, u32[]{:S(2)}, u32[]{:S(2)}) async-start(f32[8,1,32768]{2,1,0:T(1,128)} %reshape.239), calls=%async_computation.2 | async-start | bytes 2097152 | tf_op jit(solution)/shard_map/all_to_all | solution.py:131
  229.7 16.9 %copy-start.49 = (f32[16,32,128]{2,0,1:T(8,128)S(1)}, f32[16,32,128]{2,0,1:T(8,128)}, u32[]{:S(2)}) copy-start(f32[16,32,128]{2,0,1:T(8,128)} %copy-done.48) | copy-start | bytes 786436
  229.7 18.0 %copy-start.36 = (f32[16,64,128]{2,0,1:T(8,128)S(1)}, f32[16,64,128]{2,0,1:T(8,128)}, u32[]{:S(2)}) copy-start(f32[16,64,128]{2,0,1:T(8,128)} %copy-done.35) | copy-start | bytes 1572868
  229.8 18.0 %copy-start.40 = (f32[16,64,128]{2,0,1:T(8,128)S(1)}, f32[16,64,128]{2,0,1:T(8,128)}, u32[]{:S(2)}) copy-start(f32[16,64,128]{2,0,1:T(8,128)} %copy-done.39) | copy-start | bytes 1572868
  230.8 16.9 %copy-start.44 = (f32[16,64,128]{2,0,1:T(8,128)S(1)}, f32[16,64,128]{2,0,1:T(8,128)}, u32[]{:S(2)}) copy-start(f32[16,64,128]{2,0,1:T(8,128)} %copy-done.43) | copy-start | bytes 1572868
  239.9 28.2 %all-to-all-start.5 = ((f32[64,32,128]{2,1,0:T(8,128)}), f32[64,32,128]{2,1,0:T(8,128)S(1)}, u32[]{:S(2)}, u32[]{:S(2)}) async-start(f32[64,32,128]{2,1,0:T(8,128)} %bitcast.92), calls=%async_computation.5 | async-start | bytes 2097152 | tf_op jit(solution)/shard_map/all_to_all | solution.py:137
  272.3 3.0 collective-permute-start.4
  274.0 7.0 %collective-permute-start.5 = (f32[16,128,4]{1,0,2:T(8,128)S(1)}, f32[16,128,4]{1,0,2:T(8,128)S(1)}, u32[]{:S(2)}, u32[]{:S(2)}) collective-permute-start(f32[16,128,4]{1,0,2:T(8,128)S(1)} %copy.1277), channel_id=1, source_target_pairs={{4,0},{8,4},{12,8},{16,12},{20,16},{24,20},{28,24},{5,1},{9,5},{13... | collective-permute-start | bytes 98312 | tf_op jit(solution)/shard_map/ppermute | solution.py:21
  284.6 11.9 %collective-permute-start.6 = (f32[4,128,136]{2,0,1:T(4,128)}, f32[4,128,136]{2,0,1:T(4,128)S(1)}, u32[]{:S(2)}, u32[]{:S(2)}) collective-permute-start(f32[4,128,136]{2,0,1:T(4,128)} %get-tuple-element.59), channel_id=1, source_target_pairs={{0,1},{1,2},{2,3},{4,5},{5,6},{6,7},{8,9},{9,10},{10,11},{12,13},{... | collective-permute-start | bytes 835592 | tf_op jit(solution)/shard_map/ppermute | solution.py:18
  285.9 15.2 %collective-permute-start.7 = (f32[4,128,136]{2,0,1:T(4,128)}, f32[4,128,136]{2,0,1:T(4,128)S(1)}, u32[]{:S(2)}, u32[]{:S(2)}) collective-permute-start(f32[4,128,136]{2,0,1:T(4,128)} %get-tuple-element.60), channel_id=1, source_target_pairs={{1,0},{2,1},{3,2},{5,4},{6,5},{7,6},{9,8},{10,9},{11,10},{13,12},{... | collective-permute-start | bytes 835592 | tf_op jit(solution)/shard_map/ppermute | solution.py:21
  287.2 38.4 %all-to-all-start.6 = ((f32[16,128,128]{2,0,1:T(8,128)}), f32[16,128,128]{2,0,1:T(8,128)}, u32[]{:S(2)}, u32[]{:S(2)}) async-start(f32[16,128,128]{2,0,1:T(8,128)} %fusion.111), calls=%async_computation.6 | async-start | bytes 2097152 | tf_op jit(solution)/shard_map/all_to_all | solution.py:128
  325.6 20.4 %all-to-all-start.7 = ((f32[16,128,128]{2,0,1:T(8,128)}), f32[16,128,128]{2,0,1:T(8,128)S(1)}, u32[]{:S(2)}, u32[]{:S(2)}) async-start(f32[16,128,128]{2,0,1:T(8,128)} %get-tuple-element.57), calls=%async_computation.7 | async-start | bytes 2097152 | tf_op jit(solution)/shard_map/all_to_all | solution.py:127
  346.0 101.0 %all-to-all-start.9 = ((f32[16,128,128]{2,0,1:T(8,128)}), f32[16,128,128]{2,0,1:T(8,128)}, u32[]{:S(2)}, u32[]{:S(2)}) async-start(f32[16,128,128]{2,0,1:T(8,128)} %fusion.111), calls=%async_computation.9 | async-start | bytes 2097152 | tf_op jit(solution)/shard_map/all_to_all | solution.py:134
  447.0 31.2 %all-to-all-start.10 = ((f32[16,128,128]{2,0,1:T(8,128)}), f32[16,128,128]{2,0,1:T(8,128)}, u32[]{:S(2)}, u32[]{:S(2)}) async-start(f32[16,128,128]{2,0,1:T(8,128)} %get-tuple-element.58), calls=%async_computation.10 | async-start | bytes 2097152 | tf_op jit(solution)/shard_map/all_to_all | solution.py:133
  478.2 19.8 %all-to-all-start.8 = ((f32[8,1,32768]{2,1,0:T(1,128)}), f32[8,1,32768]{2,1,0:T(1,128)}, u32[]{:S(2)}, u32[]{:S(2)}) async-start(f32[8,1,32768]{2,1,0:T(1,128)} %reshape.241), calls=%async_computation.8 | async-start | bytes 2097152 | tf_op jit(solution)/shard_map/all_to_all | solution.py:131
  487.9 16.4 %copy-start.46 = (f32[16,32,128]{2,0,1:T(8,128)S(1)}, f32[16,32,128]{2,0,1:T(8,128)}, u32[]{:S(2)}) copy-start(f32[16,32,128]{2,0,1:T(8,128)} %copy-done.45) | copy-start | bytes 786436
  487.9 17.6 %copy-start.34 = (f32[16,64,128]{2,0,1:T(8,128)S(1)}, f32[16,64,128]{2,0,1:T(8,128)}, u32[]{:S(2)}) copy-start(f32[16,64,128]{2,0,1:T(8,128)} %copy-done.33) | copy-start | bytes 1572868
  487.9 17.6 %copy-start.38 = (f32[16,64,128]{2,0,1:T(8,128)S(1)}, f32[16,64,128]{2,0,1:T(8,128)}, u32[]{:S(2)}) copy-start(f32[16,64,128]{2,0,1:T(8,128)} %copy-done.37) | copy-start | bytes 1572868
  489.0 16.5 %copy-start.42 = (f32[16,64,128]{2,0,1:T(8,128)S(1)}, f32[16,64,128]{2,0,1:T(8,128)}, u32[]{:S(2)}) copy-start(f32[16,64,128]{2,0,1:T(8,128)} %copy-done.41) | copy-start | bytes 1572868
  498.0 27.9 %all-to-all-start.11 = ((f32[64,32,128]{2,1,0:T(8,128)}), f32[64,32,128]{2,1,0:T(8,128)S(1)}, u32[]{:S(2)}, u32[]{:S(2)}) async-start(f32[64,32,128]{2,1,0:T(8,128)} %bitcast.188), calls=%async_computation.11 | async-start | bytes 2097152 | tf_op jit(solution)/shard_map/all_to_all | solution.py:137
  (68 other events, 200.3 us)
where the time goes:
time: 535 us; the launch traced here: 528 us
  other arithmetic  213 us (40%)
  local copies, waits for them, and re-layouts  176 us (33%)
  starting transfers between devices  83.4 us (16%)
  waiting for transfers between devices  52.6 us (10%)
    add x40, other arithmetic, reduce_solve(): new_right = odds[3] + factor_before * before[3] + factor_after * after[3]  74.7 us
    unnamed x167, local copies, waits for them, and re-layouts  56.3 us
    slice x124, local copies, waits for them, and re-layouts, slice_axis(): lax.slice_in_dim(array, start, start + stride * (count - 1) + 1, stride,...  55.3 us
    another operation x86, other arithmetic, reduce_solve(): paired = jnp.stack([solved_even, odd_full], axis=axis + 1)  35.7 us
    mul x40, other arithmetic, reduce_solve(): new_upper = factor_after * after[2]  25 us
    neg x6, other arithmetic, line_solve(): return reduce_solve(-lower, diagonal, -upper, right, axis)  24 us
    all_to_all x2, starting transfers between devices, on_device(): lax.all_to_all(face_y, 'gy', split_axis=1, concat_axis=2, tiled=True)  20.9 us
    all_to_all x2, waiting for transfers between devices, on_device(): lax.all_to_all(lined_y, 'gy', split_axis=2, concat_axis=1, tiled=True)  18.1 us
  transfers between devices with their start and end apart: 20, of which 12 were waited for; matrix products, arithmetic and copies ran while one was open for 67% of the time, Pallas kernels for 0%

commit v1 on v0

v1 whole, which is shorter than its diff:
```python
import functools

import jax
import jax.numpy as jnp
from jax import lax
from jax.experimental import pallas as pl
from jax.experimental.pallas import tpu as pltpu
from jax.sharding import PartitionSpec as P

STEPS = 2
TAPS = (0.05448868, 0.24420134, 0.40261995, 0.24420134, 0.05448868)
SCALE = 600.0
MESH = pl.DeviceIdType.MESH
DIRECTIONS = [(dy, dz) for dz in (-1, 1, 0) for dy in (0, -1, 1) if (dy, dz) != (0, 0)]
PAD = 8
HALO = 4
CHUNK = 32
STENCIL_ROWS = 48


def merge(left, right):
    ea, ra, eb, rb, g, f = left
    ea2, ra2, eb2, rb2, g2, f2 = right
    s1 = 1.0 / (eb + g + f)
    wg, wf, q1 = g * s1, f * s1, rb * s1
    ea = ea + wg * eb
    ra = ra + wg * rb
    ea2 = ea2 + wf * eb
    ra2 = ra2 + wf * rb
    g1 = wf * g
    s2 = 1.0 / (ea2 + g1 + g2)
    vg, vf, q2 = g1 * s2, g2 * s2, ra2 * s2
    joined = (ea + vg * ea2, ra + vg * ra2, eb2 + vf * ea2, rb2 + vf * ra2, vf * g1, f2)
    return joined, (wg, wf, q1, vg, vf, q2)


def unmerge(weights, va, vb):
    wg, wf, q1, vg, vf, q2 = weights
    inner_right = vg * va + vf * vb + q2
    inner_left = wg * va + wf * inner_right + q1
    return inner_left, inner_right


def solve_pair(ea, ra, eb, rb, g):
    s = 1.0 / (ea + g)
    w = g * s
    vb = (rb + w * ra) / (eb + w * ea)
    return w * vb + ra * s, vb


def kernel(ny, nz, rounds, vol, con, out, c_ref, t_ref, b_ref, d_ref, dt_ref, wx_ref, wy_ref, wz_ref, vx_ref, vy_ref,
           vz_ref, zr_ref, zi_ref, zsend, zbuf, zvsend, zv, ysend, yrecv,
           halo_s, halo_r, zs, zrs, zvs, zvr, ys, yr):
    depth, nx, cols = vol.shape
    rows = cols + 2 * PAD
    tall = depth + 2 * HALO
    chunks = cols // CHUNK
    ky = lax.axis_index("gy")
    kz = lax.axis_index("gz")

    def at(y, z):
        return {"gy": y, "gz": z}

    def exists(dy, dz):
        ok = True
        if dy:
            ok = (ky + dy >= 0) & (ky + dy < ny)
        if dz:
            ok = ok & (kz + dz >= 0) & (kz + dz < nz)
        return ok

    def partner(r):
        size = 2 ** r
        bit = lax.rem(lax.div(ky, size), 2)
        return bit, ky + size * (1 - 2 * bit)

    barrier = pltpu.get_barrier_semaphore()
    expected = jnp.int32(rounds)
    for dy, dz in DIRECTIONS:
        ok = exists(dy, dz)
        expected = expected + jnp.where(ok, 1, 0)

        @pl.when(ok)
        def _(dy=dy, dz=dz):
            pl.semaphore_signal(barrier, inc=1, device_id=at(ky + dy, kz + dz), device_id_type=MESH)

    for r in range(rounds):
        pl.semaphore_signal(barrier, inc=1, device_id=at(partner(r)[1], kz), device_id_type=MESH)
    pl.semaphore_wait(barrier, expected)

    left = kz < nz // 2
    inward = jnp.where(left, 1, -1)
    order = jnp.where(left, kz, nz - 1 - kz)
    middle = order == nz // 2 - 1
    outermost = order == 0
    slot_out = jnp.where(middle, 1, 0)

    lane = lax.broadcasted_iota(jnp.int32, (STENCIL_ROWS, nx), 1)
    keep = {s: (lane >= s) if s > 0 else (lane < nx + s) for s in (-2, -1, 1, 2)}

    def shifted(value, s):
        return jnp.where(keep[s], pltpu.roll(value, s % nx, 1), 0.0)

    contrast = con[...]
    squared = jnp.broadcast_to(contrast * contrast, (STENCIL_ROWS, nx))
    t_ref[0:8, :] = jnp.zeros((8, nx), jnp.float32)
    t_ref[rows + 8:rows + 16, :] = jnp.zeros((8, nx), jnp.float32)
    out[...] = vol[...]

    out2 = out.reshape(depth * nx, cols)
    dt2 = dt_ref.reshape(depth * nx, cols)
    vx2 = vx_ref.reshape(depth * nx, cols)
    vy2 = vy_ref.reshape(depth * cols, nx)
    d2 = d_ref.reshape((depth + 2) * rows, nx)

    def step_body(step, carry):
        c4 = c_ref.at[step]
        c2 = c4.reshape(tall * rows, nx)

        @pl.loop(0, depth)
        def _(z):
            c4[z + HALO, PAD:PAD + cols, :] = out[z].T

        def halo(i):
            dy, dz = DIRECTIONS[i]
            src_y = {0: (PAD, cols), 1: (cols, PAD), -1: (PAD, PAD)}[dy]
            dst_y = {0: (PAD, cols), 1: (0, PAD), -1: (PAD + cols, PAD)}[dy]
            src_z = {0: (HALO, depth), 1: (depth, HALO), -1: (HALO, HALO)}[dz]
            dst_z = {0: (HALO, depth), 1: (0, HALO), -1: (HALO + depth, HALO)}[dz]
            src = c4.at[pl.ds(*src_z), pl.ds(*src_y), :]
            dst = c4.at[pl.ds(*dst_z), pl.ds(*dst_y), :]
            copy = pltpu.make_async_remote_copy(
                src_ref=src, dst_ref=dst, send_sem=halo_s.at[step, i], recv_sem=halo_r.at[step, i],
                device_id=at(ky + dy, kz + dz), device_id_type=MESH)
            return copy, dst_z, dst_y

        for i, (dy, dz) in enumerate(DIRECTIONS):
            copy, dst_z, dst_y = halo(i)

            @pl.when(exists(dy, dz))
            def _(copy=copy):
                copy.start()

            @pl.when(jnp.logical_not(exists(-dy, -dz)))
            def _(dst_z=dst_z, dst_y=dst_y):
                c4[pl.ds(*dst_z), pl.ds(*dst_y), :] = jnp.zeros((dst_z[1], dst_y[1], nx), jnp.float32)

        for i, (dy, dz) in enumerate(DIRECTIONS):
            copy = halo(i)[0]

            @pl.when(exists(-dy, -dz))
            def _(copy=copy):
                copy.wait_recv()

        for i, (dy, dz) in enumerate(DIRECTIONS):
            copy = halo(i)[0]

            @pl.when(exists(dy, dz))
            def _(copy=copy):
                copy.wait_send()

        @pl.loop(0, depth + 4)
        def _(z):
            for r0 in range(0, rows, STENCIL_ROWS):
                part = pl.ds(r0, STENCIL_ROWS)
                total = TAPS[2] * c4[z + 2, part, :]
                total = total + TAPS[1] * (c4[z + 1, part, :] + c4[z + 3, part, :])
                total = total + TAPS[0] * (c4[z, part, :] + c4[z + 4, part, :])
                t_ref[pl.ds(r0 + 8, STENCIL_ROWS), :] = total
            place_z = kz * depth + z - 2
            inside_z = (place_z >= 0) & (place_z < nz * depth)
            for r0 in range(0, rows, STENCIL_ROWS):
                def tap(o):
                    return t_ref[pl.ds(r0 + 8 + o, STENCIL_ROWS), :]
                total = TAPS[2] * tap(0) + TAPS[1] * (tap(-1) + tap(1)) + TAPS[0] * (tap(-2) + tap(2))
                blurred = (TAPS[2] * total + TAPS[1] * (shifted(total, 1) + shifted(total, -1))
                           + TAPS[0] * (shifted(total, 2) + shifted(total, -2)))
                place = lax.broadcasted_iota(jnp.int32, (STENCIL_ROWS, nx), 0) + (r0 - PAD + ky * cols)
                inside = (place >= 0) & (place < ny * cols) & inside_z
                b_ref[z, pl.ds(r0 + 8, STENCIL_ROWS), :] = jnp.where(inside, blurred, 0.0)

        @pl.loop(0, depth + 2)
        def _(z):
            for r0 in range(0, rows, STENCIL_ROWS):
                part = pl.ds(r0 + 8, STENCIL_ROWS)
                mid = b_ref[z + 1, part, :]
                grad_z = b_ref[z + 2, part, :] - b_ref[z, part, :]
                grad_y = (b_ref[z + 1, pl.ds(r0 + 9, STENCIL_ROWS), :]
                          - b_ref[z + 1, pl.ds(r0 + 7, STENCIL_ROWS), :])
                grad_x = shifted(mid, -1) - shifted(mid, 1)
                square = (grad_x * grad_x + grad_y * grad_y + grad_z * grad_z) * 0.25
                d_ref[z, pl.ds(r0, STENCIL_ROWS), :] = (SCALE * squared) / (squared + square)

        @pl.loop(0, depth)
        def _(z):
            dt_ref[z] = d_ref[z + 1, PAD:PAD + cols, :].T

        @pl.loop(0, chunks)
        def _(c):
            y0 = pl.multiple_of(c * CHUNK, CHUNK)
            part = pl.ds(y0 + PAD, CHUNK)
            own = pl.ds(y0, CHUNK)
            d = d_ref[1, part, :]
            f_lo = jnp.where(kz > 0, d_ref[0, part, :] + d, 0.0)
            d_next = d_ref[2, part, :]
            g = d + d_next
            d = d_next
            ea = jnp.ones_like(g)
            ra = c4[HALO, part, :]
            e = ea
            r = c4[HALO + 1, part, :]
            for i in range(1, depth - 1):
                d_next = d_ref[i + 2, part, :]
                f = d + d_next
                d = d_next
                s = 1.0 / (e + g + f)
                wf, wg = f * s, g * s
                wz_ref[0, i, own, :] = wf
                wz_ref[1, i, own, :] = wg
                wz_ref[2, i, own, :] = r * s
                ea = ea + wg * e
                ra = ra + wg * r
                e = 1.0 + wf * e
                r = c4[HALO + i + 1, part, :] + wf * r
                g = wf * g
            f_hi = jnp.where(kz < nz - 1, d + d_ref[depth + 1, part, :], 0.0)
            zr_ref[0, own, :] = jnp.where(left, ea, e)
            zr_ref[1, own, :] = jnp.where(left, ra, r)
            zr_ref[2, own, :] = jnp.where(left, e, ea)
            zr_ref[3, own, :] = jnp.where(left, r, ra)
            zr_ref[4, own, :] = g
            zr_ref[5, own, :] = jnp.where(left, f_hi, f_lo)

        def z_copy(c, slot):
            return pltpu.make_async_remote_copy(
                src_ref=zsend.at[step, c], dst_ref=zbuf.at[step, slot, c], send_sem=zs.at[step, c],
                recv_sem=zrs.at[step, slot, c], device_id=at(ky, kz + inward), device_id_type=MESH)

        def z_back(c):
            return pltpu.make_async_remote_copy(
                src_ref=zvsend.at[step, c], dst_ref=zv.at[step, c], send_sem=zvs.at[step, c],
                recv_sem=zvr.at[step, c], device_id=at(ky, kz - inward), device_id_type=MESH)

        def z_inward(c, carry):
            own = pl.ds(pl.multiple_of(c * CHUNK, CHUNK), CHUNK)

            @pl.when(jnp.logical_not(outermost))
            def _():
                z_copy(c, 0).wait_recv()
                zr_ref[0, own, :] += zbuf[step, 0, c, 0]
                zr_ref[1, own, :] += zbuf[step, 0, c, 1]

            eo, ro, ei, ri, g, f = [zr_ref[j, own, :] for j in range(6)]
            s = 1.0 / (eo + g)
            w = g * s
            ei = ei + w * eo
            ri = ri + w * ro
            s2 = 1.0 / (ei + f)
            u = f * s2
            zi_ref[0, own, :] = w
            zi_ref[1, own, :] = ro * s
            zi_ref[2, own, :] = ei
            zi_ref[3, own, :] = ri
            zi_ref[4, own, :] = u
            zi_ref[5, own, :] = ri * s2
            zsend[step, c, 0] = u * ei
            zsend[step, c, 1] = u * ri
            z_copy(c, slot_out).start()
            return carry

        def z_outward(c, carry):
            own = pl.ds(pl.multiple_of(c * CHUNK, CHUNK), CHUNK)

            @pl.when(middle)
            def _():
                z_copy(c, 1).wait_recv()
                zr_ref[0, own, :] = (zi_ref[3, own, :] + zbuf[step, 1, c, 1]) / (zi_ref[2, own, :] + zbuf[step, 1, c, 0])

            @pl.when(jnp.logical_not(middle))
            def _():
                z_back(c).wait_recv()
                zr_ref[0, own, :] = zi_ref[4, own, :] * zv[step, c] + zi_ref[5, own, :]

            vi = zr_ref[0, own, :]
            vo = zi_ref[0, own, :] * vi + zi_ref[1, own, :]

            @pl.when(jnp.logical_not(outermost))
            def _():
                zvsend[step, c] = vo
                z_back(c).start()

            va = jnp.where(left, vo, vi)
            v = jnp.where(left, vi, vo)
            vz_ref[0, own, :] = va
            vz_ref[depth - 1, own, :] = v
            for i in range(depth - 2, 0, -1):
                v = wz_ref[0, i, own, :] * v + (wz_ref[1, i, own, :] * va + wz_ref[2, i, own, :])
                vz_ref[i, own, :] = v
            return carry

        @pl.when(outermost)
        def _():
            lax.fori_loop(0, chunks, z_inward, 0)

        def dx(i):
            return dt2[pl.ds(i, depth, stride=nx), :]

        def rx(i):
            return out2[pl.ds(i, depth, stride=nx), :]

        def dy_(i):
            return d2[pl.ds(i + rows + PAD, depth, stride=rows), :]

        def ry(i):
            return c2[pl.ds(i + HALO * rows + PAD, depth, stride=rows), :]

        half_x = nx // 2
        half_y = cols // 2

        def x_reduce(i, state):
            el, rl, dl, er, rr, dr = state
            j = nx - 1 - i
            d1 = dx(i + 1)
            d3 = dx(j - 1)
            fl = dl + d1
            fr = dr + d3
            sl = 1.0 / (el + fl)
            sr = 1.0 / (er + fr)
            wl = fl * sl
            wr = fr * sr
            wx_ref[0, i] = wl
            wx_ref[1, i] = rl * sl
            wx_ref[0, j] = wr
            wx_ref[1, j] = rr * sr
            return (1.0 + wl * el, rx(i + 1) + wl * rl, d1, 1.0 + wr * er, rx(j - 1) + wr * rr, d3)

        def y_first(base):
            d0, d1 = dy_(base), dy_(base + 1)
            one = jnp.ones_like(d0)
            return (one, ry(base), d0 + d1, one, ry(base + 1), d1)

        def y_reduce(i, state, base):
            ea, ra, g, e, r, d = state
            d1 = dy_(base + i + 1)
            f = d + d1
            s = 1.0 / (e + g + f)
            wf, wg = f * s, g * s
            wy_ref[0, base + i] = wf
            wy_ref[1, base + i] = wg
            wy_ref[2, base + i] = r * s
            return (ea + wg * e, ra + wg * r, wf * g, 1.0 + wf * e, ry(base + i + 1) + wf * r, d1)

        def y_body(i, states):
            return tuple(y_reduce(i, s, b) for s, b in zip(states, (0, half_y)))

        low, high = lax.fori_loop(1, half_y - 1, y_body, (y_first(0), y_first(half_y)))

        def y_chain(state, f):
            ea, ra, g, e, r, d = state
            return (ea, ra, e, r, g, f)

        chain_low = y_chain(low, low[5] + dy_(half_y))
        chain_high = y_chain(high, jnp.where(ky < ny - 1, high[5] + dy_(cols), 0.0))
        chain, local_weights = merge(chain_low, chain_high)

        def y_copy(r):
            return pltpu.make_async_remote_copy(
                src_ref=ysend.at[step, r], dst_ref=yrecv.at[step, r], send_sem=ys.at[step, r],
                recv_sem=yr.at[step, r], device_id=at(partner(r)[1], kz), device_id_type=MESH)

        def y_start(r, chain):
            for j in range(6):
                ysend[step, r, j] = chain[j]
            y_copy(r).start()

        if rounds:
            y_start(0, chain)

        @pl.when(jnp.logical_not(outermost))
        def _():
            lax.fori_loop(0, chunks, z_inward, 0)

        zero = jnp.zeros((depth, cols), jnp.float32)
        state = lax.fori_loop(0, half_x - 1, x_reduce, (zero + 1.0, rx(0), dx(0), zero + 1.0, rx(nx - 1), dx(nx - 1)))
        el, rl, dl, er, rr, dr = state
        x_ends = solve_pair(el, rl, er, rr, dl + dr)

        weights = []
        for r in range(rounds):
            y_copy(r).wait_recv()
            other = tuple(yrecv[step, r, j] for j in range(6))
            first = partner(r)[0] == 0
            pair_l = tuple(jnp.where(first, a, b) for a, b in zip(chain, other))
            pair_r = tuple(jnp.where(first, b, a) for a, b in zip(chain, other))
            chain, w = merge(pair_l, pair_r)
            weights.append(w)
            if r + 1 < rounds:
                y_start(r + 1, chain)

        va, vb = solve_pair(*chain[:5])
        for r in range(rounds - 1, -1, -1):
            first = partner(r)[0] == 0
            inner_l, inner_r = unmerge(weights[r], va, vb)
            va = jnp.where(first, va, inner_r)
            vb = jnp.where(first, inner_l, vb)
        inner_l, inner_r = unmerge(local_weights, va, vb)

        def put_x(i, v):
            vx2[pl.ds(i, depth, stride=nx), :] = v

        def put_y(i, v):
            vy2[pl.ds(i, depth, stride=cols), :] = v

        put_x(half_x - 1, x_ends[0])
        put_x(half_x, x_ends[1])
        put_y(0, va)
        put_y(half_y - 1, inner_l)
        put_y(half_y, inner_r)
        put_y(cols - 1, vb)

        def x_back(k, state):
            vl, vr = state
            i = half_x - 2 - k
            j = half_x + 1 + k
            vl = wx_ref[0, i] * vl + wx_ref[1, i]
            vr = wx_ref[0, j] * vr + wx_ref[1, j]
            put_x(i, vl)
            put_x(j, vr)
            return vl, vr

        lax.fori_loop(0, half_x - 1, x_back, x_ends)

        def y_back(k, state):
            vl, vr = state
            i = half_y - 2 - k
            vl = wy_ref[0, i] * vl + (wy_ref[1, i] * va + wy_ref[2, i])
            j = i + half_y
            vr = wy_ref[0, j] * vr + (wy_ref[1, j] * inner_r + wy_ref[2, j])
            put_y(i, vl)
            put_y(j, vr)
            return vl, vr

        lax.fori_loop(0, half_y - 2, y_back, (inner_l, vb))

        lax.fori_loop(0, chunks, z_outward, 0)

        @pl.loop(0, depth)
        def _(z):
            out[z] = (vx_ref[z] + (vy_ref[z] + vz_ref[z]).T) * (1.0 / 3.0)

        for r in range(rounds):
            y_copy(r).wait_send()

        @pl.loop(0, chunks)
        def _(c):
            z_copy(c, slot_out).wait_send()

            @pl.when(jnp.logical_not(outermost))
            def _():
                z_back(c).wait_send()

        return carry

    lax.fori_loop(0, STEPS, step_body, 0)


def on_device(volume, contrast):
    depth, nx, cols = volume.shape
    ny = lax.axis_size("gy")
    nz = lax.axis_size("gz")
    rounds = ny.bit_length() - 1
    assert 2 ** rounds == ny and nz % 2 == 0 and nz >= 2
    rows = cols + 2 * PAD
    chunks = cols // CHUNK
    f32 = jnp.float32
    dma = pltpu.SemaphoreType.DMA
    count = len(DIRECTIONS)
    return pl.pallas_call(
        functools.partial(kernel, ny, nz, rounds),
        out_shape=jax.ShapeDtypeStruct(volume.shape, f32),
        in_specs=[pl.BlockSpec(memory_space=pltpu.VMEM)] * 2,
        out_specs=pl.BlockSpec(memory_space=pltpu.VMEM),
        scratch_shapes=[
            pltpu.VMEM((STEPS, depth + 2 * HALO, rows, nx), f32),
            pltpu.VMEM((rows + 16, nx), f32),
            pltpu.VMEM((depth + 4, rows + 16, nx), f32),
            pltpu.VMEM((depth + 2, rows, nx), f32),
            pltpu.VMEM((depth, nx, cols), f32),
            pltpu.VMEM((2, nx, depth, cols), f32),
            pltpu.VMEM((3, cols, depth, nx), f32),
            pltpu.VMEM((3, depth, cols, nx), f32),
            pltpu.VMEM((depth, nx, cols), f32),
            pltpu.VMEM((depth, cols, nx), f32),
            pltpu.VMEM((depth, cols, nx), f32),
            pltpu.VMEM((6, cols, nx), f32),
            pltpu.VMEM((6, cols, nx), f32),
            pltpu.VMEM((STEPS, chunks, 2, CHUNK, nx), f32),
            pltpu.VMEM((STEPS, 2, chunks, 2, CHUNK, nx), f32),
            pltpu.VMEM((STEPS, chunks, CHUNK, nx), f32),
            pltpu.VMEM((STEPS, chunks, CHUNK, nx), f32),
            pltpu.VMEM((STEPS, max(rounds, 1), 6, depth, nx), f32),
            pltpu.VMEM((STEPS, max(rounds, 1), 6, depth, nx), f32),
            dma((STEPS, count)), dma((STEPS, count)),
            dma((STEPS, chunks)), dma((STEPS, 2, chunks)),
            dma((STEPS, chunks)), dma((STEPS, chunks)),
            dma((STEPS, max(rounds, 1))), dma((STEPS, max(rounds, 1))),
        ],
        compiler_params=pltpu.CompilerParams(
            collective_id=0, has_side_effects=True, vmem_limit_bytes=48 * 2 ** 20
        ),
    )(volume, contrast.reshape(1, nx))


def solution(mesh):
    in_specs = (P("gz", None, "gy"), P())
    out_specs = P("gz", None, "gy")
    return jax.shard_map(
        on_device, mesh=mesh, in_specs=in_specs, out_specs=out_specs, check_vma=False
    )
```

time: 535 us -> 80.1 us (0.15); the launches traced: 528 us -> 79.9 us
  other arithmetic: 213 us -> 0 us
  local copies, waits for them, and re-layouts: 176 us -> 2.85 us
  starting transfers between devices: 83.4 us -> 0 us
  Pallas kernels: 0 us -> 77.1 us
  waiting for transfers between devices: 52.6 us -> 0 us
    add x44 -> x0, other arithmetic: 90.9 us -> none  [the longest x40 74.7 us: reduce_solve(): new_right = odds[3] + factor_before * before[3] + factor_after * after[3]]
    pallas_call x0 -> x1, Pallas kernels: none -> 77.1 us  [on_device(): pl.pallas_call(functools.partial(kernel, ny, nz, rounds), out_shape=jax.S...]
    all_to_all x12 -> x0, starting transfers between devices: 68.3 us -> none  [the longest x2 20.9 us: on_device(): lax.all_to_all(face_y, 'gy', split_axis=1, concat_axis=2, tiled=True)]
    slice x130 -> x0, local copies, waits for them, and re-layouts: 60.3 us -> none  [the longest x124 55.3 us: slice_axis(): lax.slice_in_dim(array, start, start + stride * (count - 1) + 1, stride,...]
    unnamed x167 -> x5, local copies, waits for them, and re-layouts: 56.3 us -> 2.85 us
    all_to_all x13 -> x0, local copies, waits for them, and re-layouts: 41.9 us -> none  [the longest x2 12.4 us: on_device(): lax.all_to_all(current, 'gy', split_axis=1, concat_axis=2, tiled=True)]
    another operation x86 -> x0, other arithmetic: 35.7 us -> none  [reduce_solve(): paired = jnp.stack([solved_even, odd_full], axis=axis + 1)]
    all_to_all x12 -> x0, waiting for transfers between devices: 30.1 us -> none  [the longest x2 18.1 us: on_device(): lax.all_to_all(lined_y, 'gy', split_axis=2, concat_axis=1, tiled=True)]
  transfers between devices with their start and end apart: 20 -> 0, of which waited for: 12 -> 0; matrix products, arithmetic and copies ran while one was open for 67% -> 0% of each run, Pallas kernels for 0% -> 0%
where the time goes in v1:
time: 80.1 us; the launch traced here: 79.9 us
  Pallas kernels  77.1 us (96%)
  local copies, waits for them, and re-layouts  2.85 us (4%)
    pallas_call x1, Pallas kernels, on_device(): pl.pallas_call(functools.partial(kernel, ny, nz, rounds), out_shape=jax.S...  77.1 us
    unnamed x5, local copies, waits for them, and re-layouts  2.85 us

profile of v1, /device:TPU:0, one launch (start us, length us, event | category | flops | bytes accessed | tf_op | source)
XLA Modules:
  0.0 79.9 jit_solution(457740466380440378)
XLA Ops:
  0.0 0.0 copy-start.1
  0.0 0.7 copy-done.1
  0.7 0.0 copy-start
  0.7 1.2 %copy-done = f32[16,128,128]{2,1,0:T(8,128)S(1)} copy-done((f32[16,128,128]{2,1,0:T(8,128)S(1)}, f32[16,128,128]{2,1,0:T(8,128)}, u32[]{:S(2)}) %copy-start) | copy-done | bytes 1048600
  1.9 77.1 %shard_map.28 = f32[16,128,128]{2,1,0:T(8,128)S(1)} custom-call(f32[16,128,128]{2,1,0:T(8,128)S(1)} %copy-done, f32[1,128]{1,0:T(1,128)S(1)} %bitcast.1), custom_call_target="tpu_custom_call" | custom-call | tf_op jit(solution)/shard_map/pallas_call | solution.py:478
  79.0 1.0 %copy.4 = f32[16,128,128]{2,1,0:T(8,128)} copy(f32[16,128,128]{2,1,0:T(8,128)S(1)} %shard_map.28) | data formatting | bytes 2097152
Async XLA Ops:
  0.0 0.7 copy-start.1
  0.7 1.2 %copy-start = (f32[16,128,128]{2,1,0:T(8,128)S(1)}, f32[16,128,128]{2,1,0:T(8,128)}, u32[]{:S(2)}) copy-start(f32[16,128,128]{2,1,0:T(8,128)} %vol.1) | copy-start | bytes 3145732

commit v2 on v1

v2 whole, which is shorter than its diff:
```python
import functools

import jax
import jax.numpy as jnp
from jax import lax
from jax.experimental import pallas as pl
from jax.experimental.pallas import tpu as pltpu
from jax.sharding import PartitionSpec as P

STEPS = 2
TAPS = (0.05448868, 0.24420134, 0.40261995, 0.24420134, 0.05448868)
SCALE = 600.0
MESH = pl.DeviceIdType.MESH
DIRECTIONS = [(dy, dz) for dz in (-1, 1, 0) for dy in (0, -1, 1) if (dy, dz) != (0, 0)]
PAD = 8
HALO = 4
CHUNK = 32
STENCIL_ROWS = 48
SEGMENTS = 4


def merge(left, right):
    ea, ra, eb, rb, g, f = left
    ea2, ra2, eb2, rb2, g2, f2 = right
    s1 = 1.0 / (eb + g + f)
    wg, wf, q1 = g * s1, f * s1, rb * s1
    ea = ea + wg * eb
    ra = ra + wg * rb
    ea2 = ea2 + wf * eb
    ra2 = ra2 + wf * rb
    g1 = wf * g
    s2 = 1.0 / (ea2 + g1 + g2)
    vg, vf, q2 = g1 * s2, g2 * s2, ra2 * s2
    joined = (ea + vg * ea2, ra + vg * ra2, eb2 + vf * ea2, rb2 + vf * ra2, vf * g1, f2)
    return joined, (wg, wf, q1, vg, vf, q2)


def unmerge(weights, va, vb):
    wg, wf, q1, vg, vf, q2 = weights
    inner_right = vg * va + vf * vb + q2
    inner_left = wg * va + wf * inner_right + q1
    return inner_left, inner_right


def solve_pair(ea, ra, eb, rb, g):
    s = 1.0 / (ea + g)
    w = g * s
    vb = (rb + w * ra) / (eb + w * ea)
    return w * vb + ra * s, vb


def merge_all(chains):
    levels = []
    while len(chains) > 1:
        pairs = [merge(chains[i], chains[i + 1]) for i in range(0, len(chains), 2)]
        chains = [p[0] for p in pairs]
        levels.append([p[1] for p in pairs])
    return chains[0], levels


def unmerge_all(levels, va, vb):
    ends = [(va, vb)]
    for level in reversed(levels):
        split = []
        for weights, (a, b) in zip(level, ends):
            inner_left, inner_right = unmerge(weights, a, b)
            split += [(a, inner_left), (inner_right, b)]
        ends = split
    return ends


def line_start(get_d, get_r, count):
    states = []
    for base in range(0, count, count // SEGMENTS):
        d0, d1 = get_d(base), get_d(base + 1)
        one = jnp.ones_like(d0)
        states.append((one, get_r(base), d0 + d1, one, get_r(base + 1), d1))
    return tuple(states)


def line_reduce(get_d, get_r, weights, count, first, last, states):
    size = count // SEGMENTS

    def body(i, states):
        new = []
        for k, (ea, ra, g, e, r, d) in enumerate(states):
            j = k * size + i
            d1 = get_d(j + 1)
            f = d + d1
            s = 1.0 / (e + g + f)
            wf, wg = f * s, g * s
            weights[0, j] = wf
            weights[1, j] = wg
            weights[2, j] = r * s
            new.append((ea + wg * e, ra + wg * r, wf * g, 1.0 + wf * e, get_r(j + 1) + wf * r, d1))
        return tuple(new)

    return lax.fori_loop(first, last, body, states)


def line_chain(get_d, states, count, edge):
    size = count // SEGMENTS
    chains = []
    for k, (ea, ra, g, e, r, d) in enumerate(states):
        f = d + get_d((k + 1) * size) if k + 1 < SEGMENTS else edge(d)
        chains.append((ea, ra, e, r, g, f))
    return merge_all(chains)


def line_back(put, weights, count, ends):
    size = count // SEGMENTS
    for k, (a, b) in enumerate(ends):
        put(k * size, a)
        put(k * size + size - 1, b)

    def body(t, values):
        new = []
        for k, v in enumerate(values):
            j = k * size + size - 2 - t
            v = weights[0, j] * v + (weights[1, j] * ends[k][0] + weights[2, j])
            put(j, v)
            new.append(v)
        return tuple(new)

    lax.fori_loop(0, size - 2, body, tuple(b for a, b in ends))


def kernel(ny, nz, rounds, vol, con, out, c_ref, t_ref, b_ref, d_ref, dt_ref, wx_ref, wy_ref, wz_ref, vx_ref, vy_ref,
           vz_ref, zr_ref, zi_ref, zsend, zbuf, zvsend, zv, ysend, yrecv,
           halo_s, halo_r, zs, zrs, zvs, zvr, ys, yr):
    depth, nx, cols = vol.shape
    rows = cols + 2 * PAD
    tall = depth + 2 * HALO
    chunks = cols // CHUNK
    ky = lax.axis_index("gy")
    kz = lax.axis_index("gz")

    def at(y, z):
        return {"gy": y, "gz": z}

    def exists(dy, dz):
        ok = True
        if dy:
            ok = (ky + dy >= 0) & (ky + dy < ny)
        if dz:
            ok = ok & (kz + dz >= 0) & (kz + dz < nz)
        return ok

    def partner(r):
        size = 2 ** r
        bit = lax.rem(lax.div(ky, size), 2)
        return bit, ky + size * (1 - 2 * bit)

    barrier = pltpu.get_barrier_semaphore()
    expected = jnp.int32(rounds)
    for dy, dz in DIRECTIONS:
        ok = exists(dy, dz)
        expected = expected + jnp.where(ok, 1, 0)

        @pl.when(ok)
        def _(dy=dy, dz=dz):
            pl.semaphore_signal(barrier, inc=1, device_id=at(ky + dy, kz + dz), device_id_type=MESH)

    for r in range(rounds):
        pl.semaphore_signal(barrier, inc=1, device_id=at(partner(r)[1], kz), device_id_type=MESH)
    @pl.loop(0, depth // 4)
    def _(k):
        for z in [4 * k, 4 * k + 1, 4 * k + 2, 4 * k + 3]:
            plane = vol[z]
            out[z] = plane
            c_ref[0, z + HALO, PAD:PAD + cols, :] = plane.T

    pl.semaphore_wait(barrier, expected)

    left = kz < nz // 2
    inward = jnp.where(left, 1, -1)
    order = jnp.where(left, kz, nz - 1 - kz)
    middle = order == nz // 2 - 1
    outermost = order == 0
    slot_out = jnp.where(middle, 1, 0)

    lane = lax.broadcasted_iota(jnp.int32, (STENCIL_ROWS, nx), 1)
    keep = {s: (lane >= s) if s > 0 else (lane < nx + s) for s in (-2, -1, 1, 2)}

    def shifted(value, s):
        return jnp.where(keep[s][:value.shape[0]], pltpu.roll(value, s % nx, 1), 0.0)

    contrast = con[...]
    squared = jnp.broadcast_to(contrast * contrast, (STENCIL_ROWS, nx))
    t_ref[0:8, :] = jnp.zeros((8, nx), jnp.float32)
    t_ref[rows + 8:rows + 16, :] = jnp.zeros((8, nx), jnp.float32)

    out2 = out.reshape(depth * nx, cols)
    dt2 = dt_ref.reshape(depth * nx, cols)
    vx2 = vx_ref.reshape(depth * nx, cols)
    vy2 = vy_ref.reshape(depth * cols, nx)
    d2 = d_ref.reshape((depth + 2) * rows, nx)

    def finish(z, target):
        plane = (vx_ref[z] + (vy_ref[z] + vz_ref[z]).T) * (1.0 / 3.0)
        out[z] = plane
        if target is not None:
            target[z + HALO, PAD:PAD + cols, :] = plane.T

    def finish_edges(target):
        @pl.loop(0, HALO // 2)
        def _(k):
            for t in range(2):
                finish(2 * k + t, target)
                finish(depth - HALO + 2 * k + t, target)

    def finish_middle(target):
        @pl.loop(0, (depth - 2 * HALO) // 4)
        def _(k):
            for t in range(4):
                finish(HALO + 4 * k + t, target)

    parts = [(r0, min(STENCIL_ROWS, cols + 8 - r0)) for r0 in range(0, cols + 8, STENCIL_ROWS)]

    for step in range(STEPS):
        c4 = c_ref.at[step]
        c2 = c4.reshape(tall * rows, nx)

        def halo(i, c4=c4, step=step):
            dy, dz = DIRECTIONS[i]
            src_y = {0: (PAD, cols), 1: (cols, PAD), -1: (PAD, PAD)}[dy]
            dst_y = {0: (PAD, cols), 1: (0, PAD), -1: (PAD + cols, PAD)}[dy]
            src_z = {0: (HALO, depth), 1: (depth, HALO), -1: (HALO, HALO)}[dz]
            dst_z = {0: (HALO, depth), 1: (0, HALO), -1: (HALO + depth, HALO)}[dz]
            src = c4.at[pl.ds(*src_z), pl.ds(*src_y), :]
            dst = c4.at[pl.ds(*dst_z), pl.ds(*dst_y), :]
            copy = pltpu.make_async_remote_copy(
                src_ref=src, dst_ref=dst, send_sem=halo_s.at[step, i], recv_sem=halo_r.at[step, i],
                device_id=at(ky + dy, kz + dz), device_id_type=MESH)
            return copy, dst_z, dst_y

        def send(layers, halo=halo, c4=c4):
            for i, (dy, dz) in enumerate(DIRECTIONS):
                if (dz != 0) != layers:
                    continue
                copy, dst_z, dst_y = halo(i)

                @pl.when(exists(dy, dz))
                def _(copy=copy):
                    copy.start()

                @pl.when(jnp.logical_not(exists(-dy, -dz)))
                def _(dst_z=dst_z, dst_y=dst_y):
                    c4[pl.ds(*dst_z), pl.ds(*dst_y), :] = jnp.zeros((dst_z[1], dst_y[1], nx), jnp.float32)

        def receive(layers):
            for i, (dy, dz) in enumerate(DIRECTIONS):
                if (dz != 0) != layers:
                    continue
                copy = halo(i)[0]

                @pl.when(exists(-dy, -dz))
                def _(copy=copy):
                    copy.wait_recv()

        if step == 0:
            send(True)
        else:
            finish_edges(c4)
            send(True)
            finish_middle(c4)
        send(False)

        def blur(z0, z1):
            @pl.loop(z0, z1)
            def _(z):
                for r0 in range(0, rows, STENCIL_ROWS):
                    part = pl.ds(r0, STENCIL_ROWS)
                    total = TAPS[2] * c4[z + 2, part, :]
                    total = total + TAPS[1] * (c4[z + 1, part, :] + c4[z + 3, part, :])
                    total = total + TAPS[0] * (c4[z, part, :] + c4[z + 4, part, :])
                    t_ref[pl.ds(r0 + 8, STENCIL_ROWS), :] = total
                for r0, size in parts:
                    def tap(o):
                        return t_ref[pl.ds(r0 + 12 + o, size), :]
                    total = TAPS[2] * tap(0) + TAPS[1] * (tap(-1) + tap(1)) + TAPS[0] * (tap(-2) + tap(2))
                    b_ref[z, pl.ds(r0, size), :] = (
                        TAPS[2] * total + TAPS[1] * (shifted(total, 1) + shifted(total, -1))
                        + TAPS[0] * (shifted(total, 2) + shifted(total, -2)))

            @pl.when(ky == 0)
            def _():
                b_ref[z0:z1, PAD - 5:PAD - 4, :] = jnp.zeros((z1 - z0, 1, nx), jnp.float32)

            @pl.when(ky == ny - 1)
            def _():
                b_ref[z0:z1, cols + PAD - 4:cols + PAD - 3, :] = jnp.zeros((z1 - z0, 1, nx), jnp.float32)

        def diffuse(z0, z1):
            @pl.loop(z0, z1)
            def _(z):
                for r0, size in parts:
                    mid = b_ref[z + 1, pl.ds(r0 + 4, size), :]
                    grad_z = b_ref[z + 2, pl.ds(r0 + 4, size), :] - b_ref[z, pl.ds(r0 + 4, size), :]
                    grad_y = b_ref[z + 1, pl.ds(r0 + 5, size), :] - b_ref[z + 1, pl.ds(r0 + 3, size), :]
                    grad_x = shifted(mid, -1) - shifted(mid, 1)
                    square = (grad_x * grad_x + grad_y * grad_y + grad_z * grad_z) * 0.25
                    d_ref[z, pl.ds(r0 + PAD, size), :] = (SCALE * squared[:size]) / (squared[:size] + square)

        def turn(z0, z1):
            step_by = 2 if (z1 - z0) % 2 == 0 else 1

            @pl.loop(0, (z1 - z0) // step_by)
            def _(k):
                for t in range(step_by):
                    z = z0 + k * step_by + t
                    dt_ref[z] = d_ref[z + 1, PAD:PAD + cols, :].T

        receive(False)
        blur(HALO, depth)
        diffuse(HALO, depth - 2)
        turn(HALO - 1, depth - 3)
        receive(True)
        blur(0, HALO)
        blur(depth, depth + 4)

        @pl.when(kz == 0)
        def _():
            b_ref[1] = jnp.zeros(b_ref.shape[1:], jnp.float32)

        @pl.when(kz == nz - 1)
        def _():
            b_ref[depth + 2] = jnp.zeros(b_ref.shape[1:], jnp.float32)

        diffuse(0, HALO)
        diffuse(depth - 2, depth + 2)
        turn(0, HALO - 1)
        turn(depth - 3, depth)

        for i, (dy, dz) in enumerate(DIRECTIONS):
            copy = halo(i)[0]

            @pl.when(exists(dy, dz))
            def _(copy=copy):
                copy.wait_send()

        def z_copy(c, slot):
            return pltpu.make_async_remote_copy(
                src_ref=zsend.at[step, c], dst_ref=zbuf.at[step, slot, c], send_sem=zs.at[step, c],
                recv_sem=zrs.at[step, slot, c], device_id=at(ky, kz + inward), device_id_type=MESH)

        def z_back(c):
            return pltpu.make_async_remote_copy(
                src_ref=zvsend.at[step, c], dst_ref=zv.at[step, c], send_sem=zvs.at[step, c],
                recv_sem=zvr.at[step, c], device_id=at(ky, kz - inward), device_id_type=MESH)

        def z_inward(c, carry):
            own = pl.ds(pl.multiple_of(c * CHUNK, CHUNK), CHUNK)

            @pl.when(jnp.logical_not(outermost))
            def _():
                z_copy(c, 0).wait_recv()
                zr_ref[0, own, :] += zbuf[step, 0, c, 0]
                zr_ref[1, own, :] += zbuf[step, 0, c, 1]

            eo, ro, ei, ri, g, f = [zr_ref[j, own, :] for j in range(6)]
            s = 1.0 / (eo + g)
            w = g * s
            ei = ei + w * eo
            ri = ri + w * ro
            s2 = 1.0 / (ei + f)
            u = f * s2
            zi_ref[0, own, :] = w
            zi_ref[1, own, :] = ro * s
            zi_ref[2, own, :] = ei
            zi_ref[3, own, :] = ri
            zi_ref[4, own, :] = u
            zi_ref[5, own, :] = ri * s2
            zsend[step, c, 0] = u * ei
            zsend[step, c, 1] = u * ri
            z_copy(c, slot_out).start()
            return carry

        def z_outward(c, carry):
            own = pl.ds(pl.multiple_of(c * CHUNK, CHUNK), CHUNK)

            @pl.when(middle)
            def _():
                z_copy(c, 1).wait_recv()
                zr_ref[0, own, :] = (zi_ref[3, own, :] + zbuf[step, 1, c, 1]) / (zi_ref[2, own, :] + zbuf[step, 1, c, 0])

            @pl.when(jnp.logical_not(middle))
            def _():
                z_back(c).wait_recv()
                zr_ref[0, own, :] = zi_ref[4, own, :] * zv[step, c] + zi_ref[5, own, :]

            vi = zr_ref[0, own, :]
            vo = zi_ref[0, own, :] * vi + zi_ref[1, own, :]

            @pl.when(jnp.logical_not(outermost))
            def _():
                zvsend[step, c] = vo
                z_back(c).start()

            va = jnp.where(left, vo, vi)
            v = jnp.where(left, vi, vo)
            vz_ref[0, own, :] = va
            vz_ref[depth - 1, own, :] = v
            for i in range(depth - 2, 0, -1):
                v = wz_ref[0, i, own, :] * v + (wz_ref[1, i, own, :] * va + wz_ref[2, i, own, :])
                vz_ref[i, own, :] = v
            return carry

        @pl.loop(0, chunks)
        def _(c):
            y0 = pl.multiple_of(c * CHUNK, CHUNK)
            part = pl.ds(y0 + PAD, CHUNK)
            own = pl.ds(y0, CHUNK)
            d = d_ref[1, part, :]
            f_lo = jnp.where(kz > 0, d_ref[0, part, :] + d, 0.0)
            d_next = d_ref[2, part, :]
            g = d + d_next
            d = d_next
            ea = jnp.ones_like(g)
            ra = c4[HALO, part, :]
            e = ea
            r = c4[HALO + 1, part, :]
            for i in range(1, depth - 1):
                d_next = d_ref[i + 2, part, :]
                f = d + d_next
                d = d_next
                s = 1.0 / (e + g + f)
                wf, wg = f * s, g * s
                wz_ref[0, i, own, :] = wf
                wz_ref[1, i, own, :] = wg
                wz_ref[2, i, own, :] = r * s
                ea = ea + wg * e
                ra = ra + wg * r
                e = 1.0 + wf * e
                r = c4[HALO + i + 1, part, :] + wf * r
                g = wf * g
            f_hi = jnp.where(kz < nz - 1, d + d_ref[depth + 1, part, :], 0.0)
            zr_ref[0, own, :] = jnp.where(left, ea, e)
            zr_ref[1, own, :] = jnp.where(left, ra, r)
            zr_ref[2, own, :] = jnp.where(left, e, ea)
            zr_ref[3, own, :] = jnp.where(left, r, ra)
            zr_ref[4, own, :] = g
            zr_ref[5, own, :] = jnp.where(left, f_hi, f_lo)

            @pl.when(outermost)
            def _():
                z_inward(c, 0)


        def dx(i):
            return dt2[pl.ds(i, depth, stride=nx), :]

        def rx(i):
            return out2[pl.ds(i, depth, stride=nx), :]

        def dy_(i):
            return d2[pl.ds(i + rows + PAD, depth, stride=rows), :]

        def ry(i):
            return c2[pl.ds(i + HALO * rows + PAD, depth, stride=rows), :]

        def put_x(i, v):
            vx2[pl.ds(i, depth, stride=nx), :] = v

        def put_y(i, v):
            vy2[pl.ds(i, depth, stride=cols), :] = v

        states = line_start(dy_, ry, cols)
        states = line_reduce(dy_, ry, wy_ref, cols, 1, cols // SEGMENTS - 1, states)
        chain, levels_y = line_chain(
            dy_, states, cols, lambda d: jnp.where(ky < ny - 1, d + dy_(cols), 0.0))

        def y_copy(r):
            return pltpu.make_async_remote_copy(
                src_ref=ysend.at[step, r], dst_ref=yrecv.at[step, r], send_sem=ys.at[step, r],
                recv_sem=yr.at[step, r], device_id=at(partner(r)[1], kz), device_id_type=MESH)

        def y_start(r, chain):
            for j in range(6):
                ysend[step, r, j] = chain[j]
            y_copy(r).start()

        if rounds:
            y_start(0, chain)

        half = nx // SEGMENTS // 2
        states = line_start(dx, rx, nx)
        states = line_reduce(dx, rx, wx_ref, nx, 1, half, states)

        @pl.when(jnp.logical_not(outermost))
        def _():
            lax.fori_loop(0, chunks, z_inward, 0)

        weights = []

        def y_round(r, chain):
            y_copy(r).wait_recv()
            other = tuple(yrecv[step, r, j] for j in range(6))
            first = partner(r)[0] == 0
            pair_l = tuple(jnp.where(first, a, b) for a, b in zip(chain, other))
            pair_r = tuple(jnp.where(first, b, a) for a, b in zip(chain, other))
            chain, w = merge(pair_l, pair_r)
            weights.append(w)
            if r + 1 < rounds:
                y_start(r + 1, chain)
            return chain

        if rounds > 0:
            chain = y_round(0, chain)
        states = line_reduce(dx, rx, wx_ref, nx, half, nx // SEGMENTS - 1, states)
        x_chain, levels_x = line_chain(dx, states, nx, jnp.zeros_like)
        if rounds > 1:
            chain = y_round(1, chain)
        line_back(put_x, wx_ref, nx, unmerge_all(levels_x, *solve_pair(*x_chain[:5])))

        @pl.when(jnp.logical_not(outermost))
        def _():
            lax.fori_loop(0, chunks, z_outward, 0)

        for r in range(2, rounds):
            chain = y_round(r, chain)

        va, vb = solve_pair(*chain[:5])
        for r in range(rounds - 1, -1, -1):
            first = partner(r)[0] == 0
            inner_l, inner_r = unmerge(weights[r], va, vb)
            va = jnp.where(first, va, inner_r)
            vb = jnp.where(first, inner_l, vb)
        line_back(put_y, wy_ref, cols, unmerge_all(levels_y, va, vb))

        @pl.when(outermost)
        def _():
            lax.fori_loop(0, chunks, z_outward, 0)

        for r in range(rounds):
            y_copy(r).wait_send()

        @pl.loop(0, chunks)
        def _(c):
            z_copy(c, slot_out).wait_send()

            @pl.when(jnp.logical_not(outermost))
            def _():
                z_back(c).wait_send()

    @pl.loop(0, depth // 4)
    def _(k):
        for t in range(4):
            finish(4 * k + t, None)


def on_device(volume, contrast):
    depth, nx, cols = volume.shape
    ny = lax.axis_size("gy")
    nz = lax.axis_size("gz")
    rounds = ny.bit_length() - 1
    assert 2 ** rounds == ny and nz % 2 == 0 and nz >= 2
    rows = cols + 2 * PAD
    chunks = cols // CHUNK
    f32 = jnp.float32
    dma = pltpu.SemaphoreType.DMA
    count = len(DIRECTIONS)
    return pl.pallas_call(
        functools.partial(kernel, ny, nz, rounds),
        out_shape=jax.ShapeDtypeStruct(volume.shape, f32),
        in_specs=[pl.BlockSpec(memory_space=pltpu.VMEM)] * 2,
        out_specs=pl.BlockSpec(memory_space=pltpu.VMEM),
        scratch_shapes=[
            pltpu.VMEM((STEPS, depth + 2 * HALO, rows, nx), f32),
            pltpu.VMEM((rows + 16, nx), f32),
            pltpu.VMEM((depth + 4, rows + 16, nx), f32),
            pltpu.VMEM((depth + 2, rows, nx), f32),
            pltpu.VMEM((depth, nx, cols), f32),
            pltpu.VMEM((3, nx, depth, cols), f32),
            pltpu.VMEM((3, cols, depth, nx), f32),
            pltpu.VMEM((3, depth, cols, nx), f32),
            pltpu.VMEM((depth, nx, cols), f32),
            pltpu.VMEM((depth, cols, nx), f32),
            pltpu.VMEM((depth, cols, nx), f32),
            pltpu.VMEM((6, cols, nx), f32),
            pltpu.VMEM((6, cols, nx), f32),
            pltpu.VMEM((STEPS, chunks, 2, CHUNK, nx), f32),
            pltpu.VMEM((STEPS, 2, chunks, 2, CHUNK, nx), f32),
            pltpu.VMEM((STEPS, chunks, CHUNK, nx), f32),
            pltpu.VMEM((STEPS, chunks, CHUNK, nx), f32),
            pltpu.VMEM((STEPS, max(rounds, 1), 6, depth, nx), f32),
            pltpu.VMEM((STEPS, max(rounds, 1), 6, depth, nx), f32),
            dma((STEPS, count)), dma((STEPS, count)),
            dma((STEPS, chunks)), dma((STEPS, 2, chunks)),
            dma((STEPS, chunks)), dma((STEPS, chunks)),
            dma((STEPS, max(rounds, 1))), dma((STEPS, max(rounds, 1))),
        ],
        compiler_params=pltpu.CompilerParams(
            collective_id=0, has_side_effects=True, vmem_limit_bytes=48 * 2 ** 20
        ),
    )(volume, contrast.reshape(1, nx))


def solution(mesh):
    in_specs = (P("gz", None, "gy"), P())
    out_specs = P("gz", None, "gy")
    return jax.shard_map(
        on_device, mesh=mesh, in_specs=in_specs, out_specs=out_specs, check_vma=False
    )
```

time: 80.1 us -> 55.8 us (0.70)
  Pallas kernels: 77.1 us -> 52.8 us
    pallas_call x1, Pallas kernels: 77.1 us -> 52.8 us  [on_device(): pl.pallas_call(functools.partial(kernel, ny, nz, rounds), out_shape=jax.S...]
where the time goes in v2:
time: 55.8 us; the launch traced here: 55.7 us
  Pallas kernels  52.8 us (95%)
  local copies, waits for them, and re-layouts  2.85 us (5%)
    pallas_call x1, Pallas kernels, on_device(): pl.pallas_call(functools.partial(kernel, ny, nz, rounds), out_shape=jax.S...  52.8 us
    unnamed x5, local copies, waits for them, and re-layouts  2.85 us

profile of v2, /device:TPU:0, one launch (start us, length us, event | category | flops | bytes accessed | tf_op | source)
XLA Modules:
  0.0 55.7 jit_solution(856858209701985521)
XLA Ops:
  0.0 0.0 copy-start.1
  0.0 0.7 %copy-done.1 = f32[128]{0:T(128)S(1)} copy-done((f32[128]{0:T(128)S(1)}, f32[128]{0:T(128)}, u32[]{:S(2)}) %copy-start.1) | copy-done | bytes 536
  0.7 0.0 copy-start
  0.7 1.2 %copy-done = f32[16,128,128]{2,1,0:T(8,128)S(1)} copy-done((f32[16,128,128]{2,1,0:T(8,128)S(1)}, f32[16,128,128]{2,1,0:T(8,128)}, u32[]{:S(2)}) %copy-start) | copy-done | bytes 1048600
  1.9 52.8 %shard_map.28 = f32[16,128,128]{2,1,0:T(8,128)S(1)} custom-call(f32[16,128,128]{2,1,0:T(8,128)S(1)} %copy-done, f32[1,128]{1,0:T(1,128)S(1)} %bitcast.1), custom_call_target="tpu_custom_call" | custom-call | tf_op jit(solution)/shard_map/pallas_call | solution.py:563
  54.7 1.0 %copy.4 = f32[16,128,128]{2,1,0:T(8,128)} copy(f32[16,128,128]{2,1,0:T(8,128)S(1)} %shard_map.28) | data formatting | bytes 2097152
Async XLA Ops:
  0.0 0.7 %copy-start.1 = (f32[128]{0:T(128)S(1)}, f32[128]{0:T(128)}, u32[]{:S(2)}) copy-start(f32[128]{0:T(128)} %param.3) | copy-start | bytes 1540
  0.7 1.2 %copy-start = (f32[16,128,128]{2,1,0:T(8,128)S(1)}, f32[16,128,128]{2,1,0:T(8,128)}, u32[]{:S(2)}) copy-start(f32[16,128,128]{2,1,0:T(8,128)} %vol.1) | copy-start | bytes 3145732

commit v3 on v2

--- a/solution.py
+++ b/solution.py
@@ -17,6 +17,7 @@
 CHUNK = 32
 STENCIL_ROWS = 48
 SEGMENTS = 4
+SKEW = 8
 
 
 def merge(left, right):
@@ -126,7 +127,7 @@
 
 
 def kernel(ny, nz, rounds, vol, con, out, c_ref, t_ref, b_ref, d_ref, dt_ref, wx_ref, wy_ref, wz_ref, vx_ref, vy_ref,
-           vz_ref, zr_ref, zi_ref, zsend, zbuf, zvsend, zv, ysend, yrecv,
+           vz_ref, cur_ref, zr_ref, zi_ref, zsend, zbuf, zvsend, zv, ysend, yrecv,
            halo_s, halo_r, zs, zrs, zvs, zvr, ys, yr):
     depth, nx, cols = vol.shape
     rows = cols + 2 * PAD
@@ -167,7 +168,7 @@
     def _(k):
         for z in [4 * k, 4 * k + 1, 4 * k + 2, 4 * k + 3]:
             plane = vol[z]
-            out[z] = plane
+            cur_ref[z, 0:nx, :] = plane
             c_ref[0, z + HALO, PAD:PAD + cols, :] = plane.T
 
     pl.semaphore_wait(barrier, expected)
@@ -187,19 +188,21 @@
 
     contrast = con[...]
     squared = jnp.broadcast_to(contrast * contrast, (STENCIL_ROWS, nx))
-    t_ref[0:8, :] = jnp.zeros((8, nx), jnp.float32)
-    t_ref[rows + 8:rows + 16, :] = jnp.zeros((8, nx), jnp.float32)
-
-    out2 = out.reshape(depth * nx, cols)
-    dt2 = dt_ref.reshape(depth * nx, cols)
-    vx2 = vx_ref.reshape(depth * nx, cols)
-    vy2 = vy_ref.reshape(depth * cols, nx)
+
+    tall_x = nx + SKEW
+    tall_y = cols + SKEW
+    cur2 = cur_ref.reshape(depth * tall_x, cols)
+    dt2 = dt_ref.reshape(depth * tall_x, cols)
+    vx2 = vx_ref.reshape(depth * tall_x, cols)
+    vy2 = vy_ref.reshape(depth * tall_y, nx)
     d2 = d_ref.reshape((depth + 2) * rows, nx)
 
     def finish(z, target):
-        plane = (vx_ref[z] + (vy_ref[z] + vz_ref[z]).T) * (1.0 / 3.0)
-        out[z] = plane
-        if target is not None:
+        plane = (vx_ref[z, 0:nx, :] + (vy_ref[z, 0:cols, :] + vz_ref[z]).T) * (1.0 / 3.0)
+        if target is None:
+            out[z] = plane
+        else:
+            cur_ref[z, 0:nx, :] = plane
             target[z + HALO, PAD:PAD + cols, :] = plane.T
 
     def finish_edges(target):
@@ -266,18 +269,22 @@
             finish_middle(c4)
         send(False)
 
+        def blur_layers(z0, z1, pieces):
+            @pl.loop(z0, z1)
+            def _(z):
+                for r0, size in pieces:
+                    part = pl.ds(r0, size)
+                    total = TAPS[2] * c4[z + 2, part, :]
+                    total = total + TAPS[1] * (c4[z + 1, part, :] + c4[z + 3, part, :])
+                    total = total + TAPS[0] * (c4[z, part, :] + c4[z + 4, part, :])
+                    t_ref[z, pl.ds(r0, size), :] = total
+
         def blur(z0, z1):
             @pl.loop(z0, z1)
             def _(z):
-                for r0 in range(0, rows, STENCIL_ROWS):
-                    part = pl.ds(r0, STENCIL_ROWS)
-                    total = TAPS[2] * c4[z + 2, part, :]
-                    total = total + TAPS[1] * (c4[z + 1, part, :] + c4[z + 3, part, :])
-                    total = total + TAPS[0] * (c4[z, part, :] + c4[z + 4, part, :])
-                    t_ref[pl.ds(r0 + 8, STENCIL_ROWS), :] = total
                 for r0, size in parts:
                     def tap(o):
-                        return t_ref[pl.ds(r0 + 12 + o, size), :]
+                        return t_ref[z, pl.ds(r0 + 4 + o, size), :]
                     total = TAPS[2] * tap(0) + TAPS[1] * (tap(-1) + tap(1)) + TAPS[0] * (tap(-2) + tap(2))
                     b_ref[z, pl.ds(r0, size), :] = (
                         TAPS[2] * total + TAPS[1] * (shifted(total, 1) + shifted(total, -1))
@@ -309,13 +316,20 @@
             def _(k):
                 for t in range(step_by):
                     z = z0 + k * step_by + t
-                    dt_ref[z] = d_ref[z + 1, PAD:PAD + cols, :].T
-
+                    dt_ref[z, 0:nx, :] = d_ref[z + 1, PAD:PAD + cols, :].T
+
+        own_rows = [(r0, min(STENCIL_ROWS, cols + PAD - r0)) for r0 in range(PAD, cols + PAD, STENCIL_ROWS)]
+        halo_rows = [(0, PAD), (cols + PAD, PAD)]
+        blur_layers(HALO, depth, own_rows)
         receive(False)
+        blur_layers(HALO, depth, halo_rows)
         blur(HALO, depth)
         diffuse(HALO, depth - 2)
         turn(HALO - 1, depth - 3)
         receive(True)
+        all_rows = own_rows + halo_rows
+        blur_layers(0, HALO, all_rows)
+        blur_layers(depth, depth + 4, all_rows)
         blur(0, HALO)
         blur(depth, depth + 4)
 
@@ -448,10 +462,10 @@
 
 
         def dx(i):
-            return dt2[pl.ds(i, depth, stride=nx), :]
+            return dt2[pl.ds(i, depth, stride=tall_x), :]
 
         def rx(i):
-            return out2[pl.ds(i, depth, stride=nx), :]
+            return cur2[pl.ds(i, depth, stride=tall_x), :]
 
         def dy_(i):
             return d2[pl.ds(i + rows + PAD, depth, stride=rows), :]
@@ -460,10 +474,10 @@
             return c2[pl.ds(i + HALO * rows + PAD, depth, stride=rows), :]
 
         def put_x(i, v):
-            vx2[pl.ds(i, depth, stride=nx), :] = v
+            vx2[pl.ds(i, depth, stride=tall_x), :] = v
 
         def put_y(i, v):
-            vy2[pl.ds(i, depth, stride=cols), :] = v
+            vy2[pl.ds(i, depth, stride=tall_y), :] = v
 
         states = line_start(dy_, ry, cols)
         states = line_reduce(dy_, ry, wy_ref, cols, 1, cols // SEGMENTS - 1, states)
@@ -483,13 +497,21 @@
         if rounds:
             y_start(0, chain)
 
-        half = nx // SEGMENTS // 2
+        size_x = nx // SEGMENTS
+        cuts = [1 + (size_x - 2) * k // chunks for k in range(chunks + 1)]
+
+        def x_piece(k, states):
+            states = line_reduce(dx, rx, wx_ref, nx, cuts[k], cuts[k + 1], states)
+
+            @pl.when(jnp.logical_not(outermost))
+            def _():
+                z_inward(k, 0)
+
+            return states
+
         states = line_start(dx, rx, nx)
-        states = line_reduce(dx, rx, wx_ref, nx, 1, half, states)
-
-        @pl.when(jnp.logical_not(outermost))
-        def _():
-            lax.fori_loop(0, chunks, z_inward, 0)
+        for k in range(chunks // 2):
+            states = x_piece(k, states)
 
         weights = []
 
@@ -507,7 +529,8 @@
 
         if rounds > 0:
             chain = y_round(0, chain)
-        states = line_reduce(dx, rx, wx_ref, nx, half, nx // SEGMENTS - 1, states)
+        for k in range(chunks // 2, chunks):
+            states = x_piece(k, states)
         x_chain, levels_x = line_chain(dx, states, nx, jnp.zeros_like)
         if rounds > 1:
             chain = y_round(1, chain)
@@ -567,16 +590,17 @@
         out_specs=pl.BlockSpec(memory_space=pltpu.VMEM),
         scratch_shapes=[
             pltpu.VMEM((STEPS, depth + 2 * HALO, rows, nx), f32),
-            pltpu.VMEM((rows + 16, nx), f32),
+            pltpu.VMEM((depth + 4, rows, nx), f32),
             pltpu.VMEM((depth + 4, rows + 16, nx), f32),
             pltpu.VMEM((depth + 2, rows, nx), f32),
-            pltpu.VMEM((depth, nx, cols), f32),
+            pltpu.VMEM((depth, nx + SKEW, cols), f32),
             pltpu.VMEM((3, nx, depth, cols), f32),
             pltpu.VMEM((3, cols, depth, nx), f32),
             pltpu.VMEM((3, depth, cols, nx), f32),
-            pltpu.VMEM((depth, nx, cols), f32),
+            pltpu.VMEM((depth, nx + SKEW, cols), f32),
+            pltpu.VMEM((depth, cols + SKEW, nx), f32),
             pltpu.VMEM((depth, cols, nx), f32),
-            pltpu.VMEM((depth, cols, nx), f32),
+            pltpu.VMEM((depth, nx + SKEW, cols), f32),
             pltpu.VMEM((6, cols, nx), f32),
             pltpu.VMEM((6, cols, nx), f32),
             pltpu.VMEM((STEPS, chunks, 2, CHUNK, nx), f32),

time: 55.8 us -> 53.5 us (0.959)
  Pallas kernels: 52.8 us -> 50.4 us
    pallas_call x1, Pallas kernels: 52.8 us -> 50.4 us  [on_device(): pl.pallas_call(functools.partial(kernel, ny, nz, rounds), out_shape=jax.S...]
where the time goes in v3:
time: 53.5 us; the launch traced here: 53.3 us
  Pallas kernels  50.4 us (94%)
  local copies, waits for them, and re-layouts  2.85 us (5%)
    pallas_call x1, Pallas kernels, on_device(): pl.pallas_call(functools.partial(kernel, ny, nz, rounds), out_shape=jax.S...  50.4 us
    unnamed x5, local copies, waits for them, and re-layouts  2.85 us

profile of v3, /device:TPU:0, one launch (start us, length us, event | category | flops | bytes accessed | tf_op | source)
XLA Modules:
  0.0 53.3 jit_solution(12777571322767916220)
XLA Ops:
  0.0 0.0 copy-start.1
  0.0 0.7 %copy-done.1 = f32[128]{0:T(128)S(1)} copy-done((f32[128]{0:T(128)S(1)}, f32[128]{0:T(128)}, u32[]{:S(2)}) %copy-start.1) | copy-done | bytes 536
  0.7 0.0 copy-start
  0.7 1.2 %copy-done = f32[16,128,128]{2,1,0:T(8,128)S(1)} copy-done((f32[16,128,128]{2,1,0:T(8,128)S(1)}, f32[16,128,128]{2,1,0:T(8,128)}, u32[]{:S(2)}) %copy-start) | copy-done | bytes 1048600
  1.9 50.4 %shard_map.28 = f32[16,128,128]{2,1,0:T(8,128)S(1)} custom-call(f32[16,128,128]{2,1,0:T(8,128)S(1)} %copy-done, f32[1,128]{1,0:T(1,128)S(1)} %bitcast.1), custom_call_target="tpu_custom_call" | custom-call | tf_op jit(solution)/shard_map/pallas_call | solution.py:586
  52.3 1.0 %copy.4 = f32[16,128,128]{2,1,0:T(8,128)} copy(f32[16,128,128]{2,1,0:T(8,128)S(1)} %shard_map.28) | data formatting | bytes 2097152
Async XLA Ops:
  0.0 0.7 %copy-start.1 = (f32[128]{0:T(128)S(1)}, f32[128]{0:T(128)}, u32[]{:S(2)}) copy-start(f32[128]{0:T(128)} %param.3) | copy-start | bytes 1540
  0.7 1.2 %copy-start = (f32[16,128,128]{2,1,0:T(8,128)S(1)}, f32[16,128,128]{2,1,0:T(8,128)}, u32[]{:S(2)}) copy-start(f32[16,128,128]{2,1,0:T(8,128)} %vol.1) | copy-start | bytes 3145732

commit v4 on v3

--- a/solution.py
+++ b/solution.py
@@ -123,7 +123,7 @@
             new.append(v)
         return tuple(new)
 
-    lax.fori_loop(0, size - 2, body, tuple(b for a, b in ends))
+    lax.fori_loop(0, size - 2, body, tuple(b for a, b in ends), unroll=3)
 
 
 def kernel(ny, nz, rounds, vol, con, out, c_ref, t_ref, b_ref, d_ref, dt_ref, wx_ref, wy_ref, wz_ref, vx_ref, vy_ref,
@@ -280,7 +280,7 @@
                     t_ref[z, pl.ds(r0, size), :] = total
 
         def blur(z0, z1):
-            @pl.loop(z0, z1)
+            @pl.loop(z0, z1, unroll=2)
             def _(z):
                 for r0, size in parts:
                     def tap(o):
@@ -299,7 +299,7 @@
                 b_ref[z0:z1, cols + PAD - 4:cols + PAD - 3, :] = jnp.zeros((z1 - z0, 1, nx), jnp.float32)
 
         def diffuse(z0, z1):
-            @pl.loop(z0, z1)
+            @pl.loop(z0, z1, unroll=2)
             def _(z):
                 for r0, size in parts:
                     mid = b_ref[z + 1, pl.ds(r0 + 4, size), :]

time: 53.5 us -> 52.1 us (0.974)
  Pallas kernels: 50.4 us -> 49.1 us
    pallas_call x1, Pallas kernels: 50.4 us -> 49.1 us  [on_device(): pl.pallas_call(functools.partial(kernel, ny, nz, rounds), out_shape=jax.S...]
where the time goes in v4:
time: 52.1 us; the launch traced here: 52 us
  Pallas kernels  49.1 us (94%)
  local copies, waits for them, and re-layouts  2.85 us (5%)
    pallas_call x1, Pallas kernels, on_device(): pl.pallas_call(functools.partial(kernel, ny, nz, rounds), out_shape=jax.S...  49.1 us
    unnamed x5, local copies, waits for them, and re-layouts  2.85 us

profile of v4, /device:TPU:0, one launch (start us, length us, event | category | flops | bytes accessed | tf_op | source)
XLA Modules:
  0.0 52.0 jit_solution(5453357296609039345)
XLA Ops:
  0.0 0.0 copy-start.1
  0.0 0.7 %copy-done.1 = f32[128]{0:T(128)S(1)} copy-done((f32[128]{0:T(128)S(1)}, f32[128]{0:T(128)}, u32[]{:S(2)}) %copy-start.1) | copy-done | bytes 536
  0.7 0.0 copy-start
  0.7 1.2 %copy-done = f32[16,128,128]{2,1,0:T(8,128)S(1)} copy-done((f32[16,128,128]{2,1,0:T(8,128)S(1)}, f32[16,128,128]{2,1,0:T(8,128)}, u32[]{:S(2)}) %copy-start) | copy-done | bytes 1048600
  1.9 49.1 %shard_map.28 = f32[16,128,128]{2,1,0:T(8,128)S(1)} custom-call(f32[16,128,128]{2,1,0:T(8,128)S(1)} %copy-done, f32[1,128]{1,0:T(1,128)S(1)} %bitcast.1), custom_call_target="tpu_custom_call" | custom-call | tf_op jit(solution)/shard_map/pallas_call | solution.py:586
  51.0 1.0 %copy.4 = f32[16,128,128]{2,1,0:T(8,128)} copy(f32[16,128,128]{2,1,0:T(8,128)S(1)} %shard_map.28) | data formatting | bytes 2097152
Async XLA Ops:
  0.0 0.7 %copy-start.1 = (f32[128]{0:T(128)S(1)}, f32[128]{0:T(128)}, u32[]{:S(2)}) copy-start(f32[128]{0:T(128)} %param.3) | copy-start | bytes 1540
  0.7 1.2 %copy-start = (f32[16,128,128]{2,1,0:T(8,128)S(1)}, f32[16,128,128]{2,1,0:T(8,128)}, u32[]{:S(2)}) copy-start(f32[16,128,128]{2,1,0:T(8,128)} %vol.1) | copy-start | bytes 3145732
